TPU v7x, 128 devices: a whole 4x4x4 slice. The times are simulated.
128 devices in a mesh: lon: 16 (over z_lo, x, core), lat: 8 (over z_hi, y).
Axes of the slice: x: 4, y: 4, z: 4 (z_hi: 2, z_lo: 2; z = z_hi * 2 + z_lo), core: 2. Of those that a mesh axis runs over, the one named last changes fastest.
Arguments:
- field: bfloat16 [32, 16384, 128], P('lat', 'lon'), may hold values from -6 to 6
- conv_weight: bfloat16 [2, 3, 3, 3, 128, 128], replicated, may hold values from -0.1875 to 0.1875
- conv_bias: float32 [2, 3, 128], replicated, may hold values from -3 to 3
- spec_real: bfloat16 [2, 128, 128, 128], P(None, 'lon'), may hold values from -1.5 to 1.5
- spec_imag: bfloat16 [2, 128, 128, 128], P(None, 'lon'), may hold values from -1.5 to 1.5
Outputs:
- result: bfloat16 [32, 16384, 128], P('lat', 'lon')
All inputs are finite; a program needn't handle non-finite values.
Results may differ from a plain program's by a relative error of at most 0.0045.
Values may be sent and summed in bfloat16 or wider, within the bound.
A program may use at most 64 MiB of HBM per device.

v0:
```python
import math

import jax
import jax.numpy as jnp
import numpy as np
from jax import lax
from jax.experimental import pallas as pl
from jax.experimental.pallas import tpu as pltpu
from jax.sharding import PartitionSpec as P

BLOCKS = 2
CONVS = 3
LON_DEVICES = 16
LAT_DEVICES = 8
CHIPS = 8
COLS = 1024
STRIPS = 16
TILES = 64
ROWS = 4
CH = 128
OWNED = 8
EXT = 70
STEP = 17
F32 = jnp.float32
BF16 = jnp.bfloat16
MESH = pl.DeviceIdType.MESH


def tables():
    total = LON_DEVICES * COLS
    tile, strip = np.meshgrid(np.arange(TILES), np.arange(STRIPS), indexing="ij")
    cell = (strip * TILES + tile).reshape(-1)
    core, chip, part, low = np.meshgrid(
        np.arange(2), np.arange(CHIPS), np.arange(2), np.arange(OWNED), indexing="ij"
    )
    mode = (OWNED * (2 * chip + core) + low).reshape(-1)
    part = part.reshape(-1)
    theta = 2.0 * np.pi / total * ((mode[:, None] * cell[None, :]) % total)
    full = np.where(part[:, None] == 0, np.cos(theta), -np.sin(theta))
    weight = np.where(mode == 0, 1.0, 2.0)[:, None] / total

    def split(table):
        table = table.astype(np.float32)
        hi = table.astype(jnp.bfloat16)
        return hi, (table - hi.astype(np.float32)).astype(jnp.bfloat16)

    forward = np.concatenate(split(full), axis=0)
    inverse = np.concatenate(split((full * weight).T), axis=1)
    phi = 2.0 * np.pi / 16.0 * ((np.arange(16)[:, None] * np.arange(OWNED)[None, :]) % 16)
    turn = np.stack([np.cos(phi), np.sin(phi)], axis=1).astype(np.float32)
    turn = np.broadcast_to(turn[..., None], (16, 2, OWNED, CH)).copy()
    return forward, inverse, turn


def split2(value):
    hi = value.astype(BF16)
    return hi, (value - hi.astype(F32)).astype(BF16)


def kernel(field, cw, cb, sr, si, ft, iv, tw, out,
           f_v, cw_v, cb_v, sr_v, si_v, ft_v, iv_v, tw_v, T, SW, X, H1, H2, H3, ST, S,
           PART, DR, RSEND, RRECV, G,
           in_sem, lon_s, lon_r, lat_s, lat_r, d_s, d_r, rs_s, rs_r, ag_s, ag_r, fw_s, fw_r):
    d = lax.axis_index("lon")
    lt = lax.axis_index("lat")
    core = lax.rem(d, 2)
    chip = lax.div(d, 2)
    sibling = chip * 2 + 1 - core
    right = lax.rem(d + 1, LON_DEVICES)
    left = lax.rem(d + LON_DEVICES - 1, LON_DEVICES)
    outer = jnp.where(core == 0, left, right)
    has_up = lt > 0
    has_down = lt < LAT_DEVICES - 1

    loads = [
        pltpu.make_async_copy(src, dst, in_sem.at[i])
        for i, (src, dst) in enumerate(
            [(field, f_v), (cw, cw_v), (cb, cb_v), (sr, sr_v), (si, si_v), (ft, ft_v),
             (iv, iv_v), (tw, tw_v)]
        )
    ]
    for load in loads:
        load.start()

    barrier = pltpu.get_barrier_semaphore()
    pl.semaphore_signal(barrier, inc=1, device_id={"lon": sibling}, device_id_type=MESH)
    pl.semaphore_signal(barrier, inc=1, device_id={"lon": outer}, device_id_type=MESH)
    for j in range(1, CHIPS):
        peer = lax.rem(chip + j, CHIPS) * 2 + core
        pl.semaphore_signal(barrier, inc=1, device_id={"lon": peer}, device_id_type=MESH)

    @pl.when(has_up)
    def _():
        pl.semaphore_signal(barrier, inc=1, device_id={"lat": lt - 1}, device_id_type=MESH)

    @pl.when(has_down)
    def _():
        pl.semaphore_signal(barrier, inc=1, device_id={"lat": lt + 1}, device_id_type=MESH)

    @pl.when(jnp.logical_not(has_up))
    def _():
        for b in range(BLOCKS):
            X[b, 0:3] = jnp.zeros((3, EXT, STRIPS, CH), BF16)

    @pl.when(jnp.logical_not(has_down))
    def _():
        for b in range(BLOCKS):
            X[b, 7:10] = jnp.zeros((3, EXT, STRIPS, CH), BF16)

    loads[0].wait()
    for row in range(ROWS):
        S[row] = f_v[row].astype(F32)
        for q in range(TILES):
            X[0, 3 + row, 3 + q] = S[row, pl.ds(q, STRIPS, stride=TILES), :].astype(BF16)

    pl.semaphore_wait(
        barrier, CHIPS + 1 + has_up.astype(jnp.int32) + has_down.astype(jnp.int32)
    )

    loads[1].wait()
    loads[2].wait()
    zero = jnp.zeros((CH, CH), BF16)

    def build(i, _):
        b = lax.div(i, CONVS)
        layer = lax.rem(i, CONVS)
        for tap in range(3):
            w0, w1, w2 = (cw_v[b, layer, a, tap] for a in range(3))
            for r, (first, second) in enumerate(((w0, zero), (w1, w0), (w2, w1), (zero, w2))):
                rows = pl.ds((tap * 4 + r) * CH, CH)
                T[i, rows, 0:CH] = first
                T[i, rows, CH:2 * CH] = second
        return 0

    lax.fori_loop(0, BLOCKS * CONVS, build, 0)

    loads[3].wait()
    loads[4].wait()

    def build_spec(i, _):
        b = lax.div(i, OWNED)
        m = lax.rem(i, OWNED)
        wr = sr_v[b, m]
        wi = si_v[b, m]
        SW[i, 0:CH, 0:CH] = wr
        SW[i, 0:CH, CH:2 * CH] = wi
        SW[i, CH:2 * CH, 0:CH] = -wi
        SW[i, CH:2 * CH, CH:2 * CH] = wr
        return 0

    lax.fori_loop(0, BLOCKS * OWNED, build_spec, 0)
    for load in loads[5:]:
        load.wait()

    cos = tw_v[d, 0]
    sin = tw_v[d, 1]
    flip = (1 - 2 * core).astype(F32)
    up_mask = has_up.astype(F32)
    down_mask = has_down.astype(F32)
    strip = lax.broadcasted_iota(jnp.int32, (STRIPS, CH), 0)
    sub = lax.rem(lax.broadcasted_iota(jnp.int32, (ROWS * OWNED, 2 * CH), 0), OWNED)

    def convolve(source, target, index, layer, b, at, to, pairs, masks):
        bias = cb_v[b, pl.ds(layer, 1), :]
        for pair in range(pairs):
            lhs = jnp.concatenate(
                [source(2 * pair + r, at + tap).reshape(STEP * STRIPS, CH)
                 for tap in range(3) for r in range(4)],
                axis=1,
            )
            total = jnp.dot(lhs, T[index], preferred_element_type=F32)
            for o in range(2):
                half = 0.5 * (total[:, o * CH:(o + 1) * CH] + bias)
                value = half * jnp.tanh(half) + half
                mask = masks.get(2 * pair + o)
                if mask is not None:
                    value = value * mask
                target[2 * pair + o, pl.ds(to, STEP)] = value.astype(BF16).reshape(
                    STEP, STRIPS, CH
                )

    def block(b, _):
        to_right = pltpu.make_async_remote_copy(
            src_ref=X.at[b, 3:7, 64:67], dst_ref=ST.at[b, 0],
            send_sem=lon_s.at[0], recv_sem=lon_r.at[b, 0],
            device_id={"lon": right}, device_id_type=MESH)
        to_left = pltpu.make_async_remote_copy(
            src_ref=X.at[b, 3:7, 3:6], dst_ref=ST.at[b, 1],
            send_sem=lon_s.at[1], recv_sem=lon_r.at[b, 1],
            device_id={"lon": left}, device_id_type=MESH)
        to_right.start()
        to_left.start()
        to_right.wait()
        to_left.wait()
        for row in range(ROWS):
            for j in range(3):
                own = X[b, 3 + row, 64 + j].astype(F32)
                other = ST[b, 0, row, j].astype(F32)
                tile = jnp.where(strip == 0, pltpu.roll(other, 1, 0), pltpu.roll(own, 1, 0))
                X[b, 3 + row, j] = tile.astype(BF16)
                own = X[b, 3 + row, 3 + j].astype(F32)
                other = ST[b, 1, row, j].astype(F32)
                tile = jnp.where(
                    strip == STRIPS - 1,
                    pltpu.roll(other, STRIPS - 1, 0), pltpu.roll(own, STRIPS - 1, 0))
                X[b, 3 + row, 67 + j] = tile.astype(BF16)

        def down_copy(first, count, slot):
            return pltpu.make_async_remote_copy(
                src_ref=X.at[b, 4:7, pl.ds(first, count)],
                dst_ref=X.at[b, 0:3, pl.ds(first, count)],
                send_sem=lat_s.at[0, slot], recv_sem=lat_r.at[b, 0, slot],
                device_id={"lat": lt + 1}, device_id_type=MESH)

        def up_copy(first, count, slot):
            return pltpu.make_async_remote_copy(
                src_ref=X.at[b, 3:6, pl.ds(first, count)],
                dst_ref=X.at[b, 7:10, pl.ds(first, count)],
                send_sem=lat_s.at[1, slot], recv_sem=lat_r.at[b, 1, slot],
                device_id={"lat": lt - 1}, device_id_type=MESH)

        pieces = [(0, 2, 4)] + [(2 + STEP * c, STEP, c) for c in range(4)]

        @pl.when(has_down)
        def _():
            for piece in pieces:
                down_copy(*piece).start()

        @pl.when(has_up)
        def _():
            for piece in pieces:
                up_copy(*piece).start()

        @pl.when(has_up)
        def _():
            down_copy(*pieces[0]).wait_recv()

        @pl.when(has_down)
        def _():
            up_copy(*pieces[0]).wait_recv()

        def chunk(c, _):
            @pl.when(has_up)
            def _():
                down_copy(2 + STEP * c, STEP, c).wait_recv()

            @pl.when(has_down)
            def _():
                up_copy(2 + STEP * c, STEP, c).wait_recv()

            base = STEP * c
            convolve(lambda r, t: X[b, r, pl.ds(t, STEP)], H1, b * CONVS, 0, b, base,
                     base + 2, 4, {0: up_mask, 1: up_mask, 6: down_mask, 7: down_mask})
            convolve(lambda r, t: H1[r, pl.ds(t, STEP)], H2, b * CONVS + 1, 1, b, base,
                     base + 2, 3, {0: up_mask, 5: down_mask})
            convolve(lambda r, t: H2[r, pl.ds(t, STEP)], H3, b * CONVS + 2, 2, b, base,
                     base, 2, {})
            return 0

        lax.fori_loop(0, 4, chunk, 0)

        for half in range(2):
            rhs = jnp.concatenate(
                [H3[2 * half + l, 4:68].reshape(COLS, CH) for l in range(2)], axis=1)
            both = jnp.dot(ft_v[...], rhs, preferred_element_type=F32)
            total = both[0:256] + both[256:512]
            for o in range(2):
                for ch in range(CHIPS):
                    first = (o * CHIPS + ch) * 16
                    for l in range(2):
                        re = total[first:first + 8, l * CH:(l + 1) * CH]
                        im = total[first + 8:first + 16, l * CH:(l + 1) * CH]
                        new_re = re * cos + im * sin
                        new_im = im * cos - re * sin
                        if o == 1:
                            new_re = new_re * flip
                            new_im = new_im * flip
                        lanes = pl.ds((2 * half + l) * CH, CH)
                        PART[o, ch, 0:8, lanes] = new_re
                        PART[o, ch, 8:16, lanes] = new_im

        swap = pltpu.make_async_remote_copy(
            src_ref=PART.at[1 - core], dst_ref=DR.at[b],
            send_sem=d_s.at[0], recv_sem=d_r.at[b],
            device_id={"lon": sibling}, device_id_type=MESH)
        swap.start()
        swap.wait()
        RSEND[...] = PART[core] + DR[b]

        def scatter(j):
            peer = lax.rem(chip + j, CHIPS)
            return pltpu.make_async_remote_copy(
                src_ref=RSEND.at[peer], dst_ref=RRECV.at[b, j - 1],
                send_sem=rs_s.at[j - 1], recv_sem=rs_r.at[b, j - 1],
                device_id={"lon": peer * 2 + core}, device_id_type=MESH)

        for j in range(1, CHIPS):
            scatter(j).start()
        spectrum = RSEND[chip]
        for j in range(1, CHIPS):
            scatter(j).wait()
        for j in range(1, CHIPS):
            spectrum = spectrum + RRECV[b, j - 1]

        lhs = jnp.concatenate(
            [jnp.concatenate([spectrum[0:8, l * CH:(l + 1) * CH],
                              spectrum[8:16, l * CH:(l + 1) * CH]], axis=1)
             for l in range(ROWS)], axis=0)
        lhs = jnp.concatenate(split2(lhs), axis=0)
        mixed = jnp.zeros((ROWS * OWNED, 2 * CH), F32)
        for m in range(OWNED):
            both = jnp.dot(lhs, SW[b * OWNED + m], preferred_element_type=F32)
            mixed = jnp.where(sub == m, both[0:32] + both[32:64], mixed)
        for l in range(ROWS):
            G[b, core, chip, :, l * CH:(l + 1) * CH] = jnp.concatenate(
                [mixed[8 * l:8 * l + 8, 0:CH], mixed[8 * l:8 * l + 8, CH:2 * CH]], axis=0
            ).astype(BF16)

        def gather(j):
            peer = lax.rem(chip + j, CHIPS)
            return pltpu.make_async_remote_copy(
                src_ref=G.at[b, core, chip], dst_ref=G.at[b, core, chip],
                send_sem=ag_s.at[j - 1], recv_sem=ag_r.at[b, j - 1],
                device_id={"lon": peer * 2 + core}, device_id_type=MESH)

        for j in range(1, CHIPS):
            gather(j).start()

        def arrived(j):
            peer = lax.rem(chip + CHIPS - j, CHIPS)
            return pltpu.make_async_remote_copy(
                src_ref=G.at[b, core, peer], dst_ref=G.at[b, core, peer],
                send_sem=ag_s.at[j - 1], recv_sem=ag_r.at[b, j - 1],
                device_id={"lon": peer * 2 + core}, device_id_type=MESH)

        for j in range(1, CHIPS):
            arrived(j).wait_recv()
        forward = pltpu.make_async_remote_copy(
            src_ref=G.at[b, core], dst_ref=G.at[b, core],
            send_sem=fw_s.at[0], recv_sem=fw_r.at[b],
            device_id={"lon": sibling}, device_id_type=MESH)
        forward.start()
        back = pltpu.make_async_remote_copy(
            src_ref=G.at[b, 1 - core], dst_ref=G.at[b, 1 - core],
            send_sem=fw_s.at[0], recv_sem=fw_r.at[b],
            device_id={"lon": sibling}, device_id_type=MESH)
        back.wait_recv()

        his = []
        los = []
        for o in range(2):
            for ch in range(CHIPS):
                parts = []
                for l in range(ROWS):
                    value = G[b, o, ch, :, l * CH:(l + 1) * CH].astype(F32)
                    re = value[0:8]
                    im = value[8:16]
                    new_re = re * cos - im * sin
                    new_im = re * sin + im * cos
                    if o == 1:
                        new_re = new_re * flip
                        new_im = new_im * flip
                    parts.append(jnp.concatenate([new_re, new_im], axis=0))
                hi, lo = split2(jnp.concatenate(parts, axis=1))
                his.append(hi)
                los.append(lo)
        hi = jnp.concatenate(his, axis=0)
        lo = jnp.concatenate(los, axis=0)
        rhs = jnp.concatenate([hi, hi, lo], axis=0)

        def finish(c, _):
            rows = pl.ds(c * 256, 256)
            table = iv_v[rows, :]
            lhs = jnp.concatenate([table, table[:, 0:256]], axis=1)
            spectral = jnp.dot(lhs, rhs, preferred_element_type=F32)
            for l in range(ROWS):
                x = X[b, 3 + l, pl.ds(3 + 16 * c, 16)].reshape(256, CH).astype(F32)
                h = H3[l, pl.ds(4 + 16 * c, 16)].reshape(256, CH).astype(F32)
                value = jnp.tanh(x + h + spectral[:, l * CH:(l + 1) * CH])
                X[b + 1, 3 + l, pl.ds(3 + 16 * c, 16)] = value.astype(BF16).reshape(
                    16, STRIPS, CH)
            return 0

        lax.fori_loop(0, 4, finish, 0)

        @pl.when(has_down)
        def _():
            for piece in pieces:
                down_copy(*piece).wait_send()

        @pl.when(has_up)
        def _():
            for piece in pieces:
                up_copy(*piece).wait_send()

        for j in range(1, CHIPS):
            gather(j).wait_send()
        forward.wait_send()
        return 0

    lax.fori_loop(0, BLOCKS, block, 0)

    for row in range(ROWS):
        for q in range(TILES):
            S[row, pl.ds(q, STRIPS, stride=TILES), :] = X[BLOCKS, 3 + row, 3 + q].astype(F32)
        f_v[row] = S[row].astype(BF16)
    store = pltpu.make_async_copy(f_v, out, in_sem.at[0])
    store.start()
    store.wait()


def per_device(field, conv_weight, conv_bias, spec_real, spec_imag):
    forward, inverse, turn = tables()
    args = (field, conv_weight, conv_bias, spec_real, spec_imag,
            jnp.asarray(forward), jnp.asarray(inverse), jnp.asarray(turn))
    tile = (STRIPS, CH)
    dma = pltpu.SemaphoreType.DMA
    return pl.pallas_call(
        kernel,
        out_shape=jax.ShapeDtypeStruct(field.shape, BF16),
        in_specs=[pl.BlockSpec(memory_space=pl.ANY)] * len(args),
        out_specs=pl.BlockSpec(memory_space=pl.ANY),
        scratch_shapes=[pltpu.VMEM(a.shape, a.dtype) for a in args] + [
            pltpu.VMEM((BLOCKS * CONVS, 12 * CH, 2 * CH), BF16),
            pltpu.VMEM((BLOCKS * OWNED, 2 * CH, 2 * CH), BF16),
            pltpu.VMEM((BLOCKS + 1, 10, EXT) + tile, BF16),
            pltpu.VMEM((8, EXT) + tile, BF16),
            pltpu.VMEM((6, EXT) + tile, BF16),
            pltpu.VMEM((4, EXT) + tile, BF16),
            pltpu.VMEM((BLOCKS, 2, ROWS, 3) + tile, BF16),
            pltpu.VMEM((ROWS, COLS, CH), F32),
            pltpu.VMEM((2, CHIPS, 16, ROWS * CH), F32),
            pltpu.VMEM((BLOCKS, CHIPS, 16, ROWS * CH), F32),
            pltpu.VMEM((CHIPS, 16, ROWS * CH), F32),
            pltpu.VMEM((BLOCKS, CHIPS - 1, 16, ROWS * CH), F32),
            pltpu.VMEM((BLOCKS, 2, CHIPS, 16, ROWS * CH), BF16),
            dma((8,)), dma((2,)), dma((BLOCKS, 2)), dma((2, 5)), dma((BLOCKS, 2, 5)),
            dma((1,)), dma((BLOCKS,)),
            dma((CHIPS - 1,)), dma((BLOCKS, CHIPS - 1)),
            dma((CHIPS - 1,)), dma((BLOCKS, CHIPS - 1)),
            dma((1,)), dma((BLOCKS,)),
        ],
        compiler_params=pltpu.CompilerParams(
            collective_id=0, has_side_effects=True, vmem_limit_bytes=62 * 1024 * 1024),
    )(*args)


def solution(mesh):
    return jax.shard_map(
        per_device,
        mesh=mesh,
        in_specs=(
            P("lat", "lon", None),
            P(),
            P(),
            P(None, "lon", None, None),
            P(None, "lon", None, None),
        ),
        out_specs=P("lat", "lon", None),
        check_vma=False,
    )
```

profile of v0, /device:TPU:25, one launch (start us, length us, event | category | flops | bytes accessed | tf_op | source)
XLA Modules:
  0.0 97.8 jit_solution(17777394819553472783)
XLA Ops:
  0.0 1.3 %copy.9.cb = f32[2,3,128]{2,1,0:T(4,128)} copy(f32[2,3,128]{2,0,1:T(2,128)} %param.10) | data formatting | bytes 6144 | tf_op args[2]
  1.3 94.3 %shard_map.82 = bf16[4,1024,128]{2,1,0:T(8,128)(2,1)} custom-call(bf16[4,1024,128]{2,1,0:T(8,128)(2,1)} %field.1, bf16[2,3,3,3,128,128]{5,4,3,2,1,0:T(8,128)(2,1)} %cw.1, f32[2,3,128]{2,1,0:T(4,128)} %copy.9.cb, bf16[2,8,128,128]{3,2,1,0:T(8,128)(2,1)} %sr.1, bf16[2,8,128,128]{3,2,1,0:T(8,128)(2,1)} %si.1, bf16[512,1024]{1,0:T(8,128)(2,1)} %constant.6.clone.ft, ...), custom_call_target="tpu_custom_call" | custom-call | tf_op jit(solution)/shard_map/pallas_call | solution.py:418
  95.6 2.3 %copy.11 = bf16[4,1024,128]{2,1,0:T(8,128)(2,1)} copy(bf16[4,1024,128]{2,1,0:T(8,128)(2,1)} %shard_map.82) | data formatting | bytes 2097152
where the time goes:
time: 98 us; the launch traced here: 97.8 us
  Pallas kernels  94.3 us (96%)
  local copies, waits for them, and re-layouts  3.54 us (4%)
    pallas_call x1, Pallas kernels, per_device(): pl.pallas_call(kernel, out_shape=jax.ShapeDtypeStruct(field.shape, BF16),...  94.3 us
    unnamed x2, local copies, waits for them, and re-layouts  3.54 us

commit v1 on v0

--- a/solution.py
+++ b/solution.py
@@ -1,4 +1,4 @@
-import math
+import contextlib
 
 import jax
 import jax.numpy as jnp
@@ -26,6 +26,10 @@
 MESH = pl.DeviceIdType.MESH
 
 
+def scope(name):
+    return contextlib.nullcontext()
+
+
 def tables():
     total = LON_DEVICES * COLS
     tile, strip = np.meshgrid(np.arange(TILES), np.arange(STRIPS), indexing="ij")
@@ -107,51 +111,55 @@
         for b in range(BLOCKS):
             X[b, 7:10] = jnp.zeros((3, EXT, STRIPS, CH), BF16)
 
-    loads[0].wait()
-    for row in range(ROWS):
-        S[row] = f_v[row].astype(F32)
-        for q in range(TILES):
-            X[0, 3 + row, 3 + q] = S[row, pl.ds(q, STRIPS, stride=TILES), :].astype(BF16)
-
-    pl.semaphore_wait(
-        barrier, CHIPS + 1 + has_up.astype(jnp.int32) + has_down.astype(jnp.int32)
-    )
-
-    loads[1].wait()
-    loads[2].wait()
-    zero = jnp.zeros((CH, CH), BF16)
-
-    def build(i, _):
-        b = lax.div(i, CONVS)
-        layer = lax.rem(i, CONVS)
-        for tap in range(3):
-            w0, w1, w2 = (cw_v[b, layer, a, tap] for a in range(3))
-            for r, (first, second) in enumerate(((w0, zero), (w1, w0), (w2, w1), (zero, w2))):
-                rows = pl.ds((tap * 4 + r) * CH, CH)
-                T[i, rows, 0:CH] = first
-                T[i, rows, CH:2 * CH] = second
-        return 0
-
-    lax.fori_loop(0, BLOCKS * CONVS, build, 0)
-
-    loads[3].wait()
-    loads[4].wait()
-
-    def build_spec(i, _):
-        b = lax.div(i, OWNED)
-        m = lax.rem(i, OWNED)
-        wr = sr_v[b, m]
-        wi = si_v[b, m]
-        SW[i, 0:CH, 0:CH] = wr
-        SW[i, 0:CH, CH:2 * CH] = wi
-        SW[i, CH:2 * CH, 0:CH] = -wi
-        SW[i, CH:2 * CH, CH:2 * CH] = wr
-        return 0
-
-    lax.fori_loop(0, BLOCKS * OWNED, build_spec, 0)
-    for load in loads[5:]:
-        load.wait()
-
+    with scope("permute_in"):
+        loads[0].wait()
+        for row in range(ROWS):
+            S[row] = f_v[row].astype(F32)
+            for q in range(TILES):
+                X[0, 3 + row, 3 + q] = S[row, pl.ds(q, STRIPS, stride=TILES), :].astype(BF16)
+
+    with scope("barrier"):
+        pl.semaphore_wait(
+            barrier, CHIPS + 1 + has_up.astype(jnp.int32) + has_down.astype(jnp.int32)
+        )
+
+    def build_weights():
+        loads[1].wait()
+        loads[2].wait()
+        zero = jnp.zeros((CH, CH), BF16)
+
+        def build(i, _):
+            b = lax.div(i, CONVS)
+            layer = lax.rem(i, CONVS)
+            for tap in range(3):
+                w0, w1, w2 = (cw_v[b, layer, a, tap] for a in range(3))
+                for r, (first, second) in enumerate(((w0, zero), (w1, w0), (w2, w1), (zero, w2))):
+                    rows = pl.ds((tap * 4 + r) * CH, CH)
+                    T[i, rows, 0:CH] = first
+                    T[i, rows, CH:2 * CH] = second
+            return 0
+
+        lax.fori_loop(0, BLOCKS * CONVS, build, 0)
+
+        loads[3].wait()
+        loads[4].wait()
+
+        def build_spec(i, _):
+            b = lax.div(i, OWNED)
+            m = lax.rem(i, OWNED)
+            wr = sr_v[b, m]
+            wi = si_v[b, m]
+            SW[i, 0:CH, 0:CH] = wr
+            SW[i, 0:CH, CH:2 * CH] = wi
+            SW[i, CH:2 * CH, 0:CH] = -wi
+            SW[i, CH:2 * CH, CH:2 * CH] = wr
+            return 0
+
+        lax.fori_loop(0, BLOCKS * OWNED, build_spec, 0)
+        for load in loads[5:7]:
+            load.wait()
+
+    loads[7].wait()
     cos = tw_v[d, 0]
     sin = tw_v[d, 1]
     flip = (1 - 2 * core).astype(F32)
@@ -161,13 +169,11 @@
     sub = lax.rem(lax.broadcasted_iota(jnp.int32, (ROWS * OWNED, 2 * CH), 0), OWNED)
 
     def convolve(source, target, index, layer, b, at, to, pairs, masks):
-        bias = cb_v[b, pl.ds(layer, 1), :]
+        bias = cb_v[layer, pl.ds(b, 1), :]
         for pair in range(pairs):
             lhs = jnp.concatenate(
                 [source(2 * pair + r, at + tap).reshape(STEP * STRIPS, CH)
-                 for tap in range(3) for r in range(4)],
-                axis=1,
-            )
+                 for tap in range(3) for r in range(4)], axis=1)
             total = jnp.dot(lhs, T[index], preferred_element_type=F32)
             for o in range(2):
                 half = 0.5 * (total[:, o * CH:(o + 1) * CH] + bias)
@@ -178,6 +184,10 @@
                 target[2 * pair + o, pl.ds(to, STEP)] = value.astype(BF16).reshape(
                     STEP, STRIPS, CH
                 )
+
+    def result(c):
+        return pltpu.make_async_copy(
+            X.at[BLOCKS, 3:7, pl.ds(3 + 16 * c, 16)], out.at[:, pl.ds(16 * c, 16)], in_sem.at[c])
 
     def block(b, _):
         to_right = pltpu.make_async_remote_copy(
@@ -190,21 +200,6 @@
             device_id={"lon": left}, device_id_type=MESH)
         to_right.start()
         to_left.start()
-        to_right.wait()
-        to_left.wait()
-        for row in range(ROWS):
-            for j in range(3):
-                own = X[b, 3 + row, 64 + j].astype(F32)
-                other = ST[b, 0, row, j].astype(F32)
-                tile = jnp.where(strip == 0, pltpu.roll(other, 1, 0), pltpu.roll(own, 1, 0))
-                X[b, 3 + row, j] = tile.astype(BF16)
-                own = X[b, 3 + row, 3 + j].astype(F32)
-                other = ST[b, 1, row, j].astype(F32)
-                tile = jnp.where(
-                    strip == STRIPS - 1,
-                    pltpu.roll(other, STRIPS - 1, 0), pltpu.roll(own, STRIPS - 1, 0))
-                X[b, 3 + row, 67 + j] = tile.astype(BF16)
-
         def down_copy(first, count, slot):
             return pltpu.make_async_remote_copy(
                 src_ref=X.at[b, 4:7, pl.ds(first, count)],
@@ -219,72 +214,107 @@
                 send_sem=lat_s.at[1, slot], recv_sem=lat_r.at[b, 1, slot],
                 device_id={"lat": lt - 1}, device_id_type=MESH)
 
-        pieces = [(0, 2, 4)] + [(2 + STEP * c, STEP, c) for c in range(4)]
-
-        @pl.when(has_down)
-        def _():
-            for piece in pieces:
-                down_copy(*piece).start()
-
-        @pl.when(has_up)
-        def _():
-            for piece in pieces:
-                up_copy(*piece).start()
-
-        @pl.when(has_up)
-        def _():
-            down_copy(*pieces[0]).wait_recv()
-
-        @pl.when(has_down)
-        def _():
-            up_copy(*pieces[0]).wait_recv()
-
-        def chunk(c, _):
+        pieces = [(17, 19, 0), (36, 17, 1), (53, 17, 2), (0, 17, 3)]
+
+        def start(some):
+            @pl.when(has_down)
+            def _():
+                for piece in some:
+                    down_copy(*piece).start()
+
             @pl.when(has_up)
             def _():
-                down_copy(2 + STEP * c, STEP, c).wait_recv()
+                for piece in some:
+                    up_copy(*piece).start()
+
+        start(pieces[:2])
+        with scope("lonwait"):
+            to_right.wait()
+            to_left.wait()
+        with scope("halo"):
+            for row in range(ROWS):
+                for j in range(3):
+                    own = X[b, 3 + row, 64 + j].astype(F32)
+                    other = ST[b, 0, row, j].astype(F32)
+                    tile = jnp.where(strip == 0, pltpu.roll(other, 1, 0), pltpu.roll(own, 1, 0))
+                    X[b, 3 + row, j] = tile.astype(BF16)
+                    own = X[b, 3 + row, 3 + j].astype(F32)
+                    other = ST[b, 1, row, j].astype(F32)
+                    tile = jnp.where(
+                        strip == STRIPS - 1,
+                        pltpu.roll(other, STRIPS - 1, 0), pltpu.roll(own, STRIPS - 1, 0))
+                    X[b, 3 + row, 67 + j] = tile.astype(BF16)
+        start(pieces[2:])
+
+        @pl.when(b == 0)
+        def _():
+            with scope("build"):
+                build_weights()
+
+        def arrive(first, count, slot):
+            @pl.when(has_up)
+            def _():
+                down_copy(first, count, slot).wait_recv()
 
             @pl.when(has_down)
             def _():
-                up_copy(2 + STEP * c, STEP, c).wait_recv()
-
-            base = STEP * c
-            convolve(lambda r, t: X[b, r, pl.ds(t, STEP)], H1, b * CONVS, 0, b, base,
-                     base + 2, 4, {0: up_mask, 1: up_mask, 6: down_mask, 7: down_mask})
-            convolve(lambda r, t: H1[r, pl.ds(t, STEP)], H2, b * CONVS + 1, 1, b, base,
-                     base + 2, 3, {0: up_mask, 5: down_mask})
-            convolve(lambda r, t: H2[r, pl.ds(t, STEP)], H3, b * CONVS + 2, 2, b, base,
-                     base, 2, {})
+                up_copy(first, count, slot).wait_recv()
+
+        def chunk(c, _):
+            with scope("latwait"):
+                @pl.when(c == 0)
+                def _():
+                    arrive(*pieces[0])
+
+                @pl.when(c > 0)
+                def _():
+                    arrive(jnp.where(c == 3, 0, 19 + STEP * c), STEP, c)
+
+            last = (c == 3).astype(jnp.int32)
+            s1 = jnp.where(c == 3, 1, 18 + STEP * c)
+            s2 = s1 - 1 + 2 * last
+            s3 = s1 - 2 + 4 * last
+            with scope("conv1"):
+                convolve(lambda r, t: X[b, r, pl.ds(t, STEP)], H1, b * CONVS, 0, b, s1 - 1, s1, 4,
+                         {0: up_mask, 1: up_mask, 6: down_mask, 7: down_mask})
+            with scope("conv2"):
+                convolve(lambda r, t: H1[r, pl.ds(t, STEP)], H2, b * CONVS + 1, 1, b, s2 - 1, s2, 3,
+                         {0: up_mask, 5: down_mask})
+            with scope("conv3"):
+                convolve(lambda r, t: H2[r, pl.ds(t, STEP)], H3, b * CONVS + 2, 2, b, s3 - 1, s3, 2,
+                         {})
             return 0
 
         lax.fori_loop(0, 4, chunk, 0)
 
-        for half in range(2):
-            rhs = jnp.concatenate(
-                [H3[2 * half + l, 4:68].reshape(COLS, CH) for l in range(2)], axis=1)
-            both = jnp.dot(ft_v[...], rhs, preferred_element_type=F32)
-            total = both[0:256] + both[256:512]
-            for o in range(2):
-                for ch in range(CHIPS):
-                    first = (o * CHIPS + ch) * 16
-                    for l in range(2):
-                        re = total[first:first + 8, l * CH:(l + 1) * CH]
-                        im = total[first + 8:first + 16, l * CH:(l + 1) * CH]
-                        new_re = re * cos + im * sin
-                        new_im = im * cos - re * sin
-                        if o == 1:
-                            new_re = new_re * flip
-                            new_im = new_im * flip
-                        lanes = pl.ds((2 * half + l) * CH, CH)
-                        PART[o, ch, 0:8, lanes] = new_re
-                        PART[o, ch, 8:16, lanes] = new_im
+        with scope("dft"):
+            for half in range(2):
+                rhs = jnp.concatenate(
+                    [H3[2 * half + l, 3:67].reshape(COLS, CH) for l in range(2)], axis=1)
+                both = jnp.dot(ft_v[...], rhs, preferred_element_type=F32)
+                total = both[0:256] + both[256:512]
+                for o in range(2):
+                    for ch in range(CHIPS):
+                        first = (o * CHIPS + ch) * 16
+                        for l in range(2):
+                            re = total[first:first + 8, l * CH:(l + 1) * CH]
+                            im = total[first + 8:first + 16, l * CH:(l + 1) * CH]
+                            new_re = re * cos + im * sin
+                            new_im = im * cos - re * sin
+                            if o == 1:
+                                new_re = new_re * flip
+                                new_im = new_im * flip
+                            lanes = pl.ds((2 * half + l) * CH, CH)
+                            PART[o, ch, 0:8, lanes] = new_re
+                            PART[o, ch, 8:16, lanes] = new_im
 
         swap = pltpu.make_async_remote_copy(
             src_ref=PART.at[1 - core], dst_ref=DR.at[b],
             send_sem=d_s.at[0], recv_sem=d_r.at[b],
             device_id={"lon": sibling}, device_id_type=MESH)
         swap.start()
-        swap.wait()
+        with scope("swapwait"):
+            swap.wait()
         RSEND[...] = PART[core] + DR[b]
 
         def scatter(j):
@@ -297,24 +327,26 @@
         for j in range(1, CHIPS):
             scatter(j).start()
         spectrum = RSEND[chip]
-        for j in range(1, CHIPS):
-            scatter(j).wait()
+        with scope("rswait"):
+            for j in range(1, CHIPS):
+                scatter(j).wait()
         for j in range(1, CHIPS):
             spectrum = spectrum + RRECV[b, j - 1]
 
-        lhs = jnp.concatenate(
-            [jnp.concatenate([spectrum[0:8, l * CH:(l + 1) * CH],
-                              spectrum[8:16, l * CH:(l + 1) * CH]], axis=1)
-             for l in range(ROWS)], axis=0)
-        lhs = jnp.concatenate(split2(lhs), axis=0)
-        mixed = jnp.zeros((ROWS * OWNED, 2 * CH), F32)
-        for m in range(OWNED):
-            both = jnp.dot(lhs, SW[b * OWNED + m], preferred_element_type=F32)
-            mixed = jnp.where(sub == m, both[0:32] + both[32:64], mixed)
-        for l in range(ROWS):
-            G[b, core, chip, :, l * CH:(l + 1) * CH] = jnp.concatenate(
-                [mixed[8 * l:8 * l + 8, 0:CH], mixed[8 * l:8 * l + 8, CH:2 * CH]], axis=0
-            ).astype(BF16)
+        with scope("mix"):
+            lhs = jnp.concatenate(
+                [jnp.concatenate([spectrum[0:8, l * CH:(l + 1) * CH],
+                                  spectrum[8:16, l * CH:(l + 1) * CH]], axis=1)
+                 for l in range(ROWS)], axis=0)
+            lhs = jnp.concatenate(split2(lhs), axis=0)
+            mixed = jnp.zeros((ROWS * OWNED, 2 * CH), F32)
+            for m in range(OWNED):
+                both = jnp.dot(lhs, SW[b * OWNED + m], preferred_element_type=F32)
+                mixed = jnp.where(sub == m, both[0:32] + both[32:64], mixed)
+            for l in range(ROWS):
+                G[b, core, chip, :, l * CH:(l + 1) * CH] = jnp.concatenate(
+                    [mixed[8 * l:8 * l + 8, 0:CH], mixed[8 * l:8 * l + 8, CH:2 * CH]], axis=0
+                ).astype(BF16)
 
         def gather(j):
             peer = lax.rem(chip + j, CHIPS)
@@ -333,8 +365,9 @@
                 send_sem=ag_s.at[j - 1], recv_sem=ag_r.at[b, j - 1],
                 device_id={"lon": peer * 2 + core}, device_id_type=MESH)
 
-        for j in range(1, CHIPS):
-            arrived(j).wait_recv()
+        with scope("agwait"):
+            for j in range(1, CHIPS):
+                arrived(j).wait_recv()
         forward = pltpu.make_async_remote_copy(
             src_ref=G.at[b, core], dst_ref=G.at[b, core],
             send_sem=fw_s.at[0], recv_sem=fw_r.at[b],
@@ -344,7 +377,8 @@
             src_ref=G.at[b, 1 - core], dst_ref=G.at[b, 1 - core],
             send_sem=fw_s.at[0], recv_sem=fw_r.at[b],
             device_id={"lon": sibling}, device_id_type=MESH)
-        back.wait_recv()
+        with scope("fwwait"):
+            back.wait_recv()
 
         his = []
         los = []
@@ -375,13 +409,19 @@
             spectral = jnp.dot(lhs, rhs, preferred_element_type=F32)
             for l in range(ROWS):
                 x = X[b, 3 + l, pl.ds(3 + 16 * c, 16)].reshape(256, CH).astype(F32)
-                h = H3[l, pl.ds(4 + 16 * c, 16)].reshape(256, CH).astype(F32)
+                h = H3[l, pl.ds(3 + 16 * c, 16)].reshape(256, CH).astype(F32)
                 value = jnp.tanh(x + h + spectral[:, l * CH:(l + 1) * CH])
                 X[b + 1, 3 + l, pl.ds(3 + 16 * c, 16)] = value.astype(BF16).reshape(
                     16, STRIPS, CH)
+
+            @pl.when(b == BLOCKS - 1)
+            def _():
+                result(c).start()
+
             return 0
 
-        lax.fori_loop(0, 4, finish, 0)
+        with scope("finish"):
+            lax.fori_loop(0, 4, finish, 0)
 
         @pl.when(has_down)
         def _():
@@ -400,24 +440,24 @@
 
     lax.fori_loop(0, BLOCKS, block, 0)
 
-    for row in range(ROWS):
-        for q in range(TILES):
-            S[row, pl.ds(q, STRIPS, stride=TILES), :] = X[BLOCKS, 3 + row, 3 + q].astype(F32)
-        f_v[row] = S[row].astype(BF16)
-    store = pltpu.make_async_copy(f_v, out, in_sem.at[0])
-    store.start()
-    store.wait()
+    with scope("store"):
+        for c in range(4):
+            result(c).wait()
+
+
+def restore(strips):
+    return jnp.transpose(strips, (0, 2, 1, 3)).reshape(ROWS, COLS, CH)
 
 
 def per_device(field, conv_weight, conv_bias, spec_real, spec_imag):
     forward, inverse, turn = tables()
-    args = (field, conv_weight, conv_bias, spec_real, spec_imag,
+    args = (field, conv_weight, jnp.transpose(conv_bias, (1, 0, 2)), spec_real, spec_imag,
             jnp.asarray(forward), jnp.asarray(inverse), jnp.asarray(turn))
     tile = (STRIPS, CH)
     dma = pltpu.SemaphoreType.DMA
-    return pl.pallas_call(
+    strips = pl.pallas_call(
         kernel,
-        out_shape=jax.ShapeDtypeStruct(field.shape, BF16),
+        out_shape=jax.ShapeDtypeStruct((ROWS, TILES) + tile, BF16),
         in_specs=[pl.BlockSpec(memory_space=pl.ANY)] * len(args),
         out_specs=pl.BlockSpec(memory_space=pl.ANY),
         scratch_shapes=[pltpu.VMEM(a.shape, a.dtype) for a in args] + [
@@ -443,6 +483,7 @@
         compiler_params=pltpu.CompilerParams(
             collective_id=0, has_side_effects=True, vmem_limit_bytes=62 * 1024 * 1024),
     )(*args)
+    return restore(strips)
 
 
 def solution(mesh):

time: 98 us -> 89.3 us (0.911)
  Pallas kernels: 94.3 us -> 86.7 us
  local copies, waits for them, and re-layouts: 3.54 us -> 2.47 us
    pallas_call x1, Pallas kernels: 94.3 us -> 86.7 us  [per_device(): pl.pallas_call(kernel, out_shape=jax.ShapeDtypeStruct((ROWS, TILES) + til...]
    unnamed x2 -> x0, local copies, waits for them, and re-layouts: 3.54 us -> none
    transpose x0 -> x1, local copies, waits for them, and re-layouts: none -> 2.47 us  [restore(): return jnp.transpose(strips, (0, 2, 1, 3)).reshape(ROWS, COLS, CH)]
where the time goes in v1:
time: 89.3 us; the launch traced here: 89.1 us
  Pallas kernels  86.7 us (97%)
  local copies, waits for them, and re-layouts  2.47 us (3%)
    pallas_call x1, Pallas kernels, per_device(): pl.pallas_call(kernel, out_shape=jax.ShapeDtypeStruct((ROWS, TILES) + til...  86.7 us
    transpose x1, local copies, waits for them, and re-layouts, restore(): return jnp.transpose(strips, (0, 2, 1, 3)).reshape(ROWS, COLS, CH)  2.47 us

profile of v1, /device:TPU:25, one launch (start us, length us, event | category | flops | bytes accessed | tf_op | source)
XLA Modules:
  0.0 89.1 jit_solution(8680111350315155075)
XLA Ops:
  0.0 86.7 %shard_map.82 = bf16[4,64,16,128]{3,2,1,0:T(8,128)(2,1)} custom-call(bf16[4,1024,128]{2,1,0:T(8,128)(2,1)} %field.1, bf16[2,3,3,3,128,128]{5,4,3,2,1,0:T(8,128)(2,1)} %cw.1, f32[3,2,128]{2,1,0:T(2,128)} %bitcast.4, bf16[2,8,128,128]{3,2,1,0:T(8,128)(2,1)} %sr.1, bf16[2,8,128,128]{3,2,1,0:T(8,128)(2,1)} %si.1, bf16[512,1024]{1,0:T(8,128)(2,1)} %constant.6.clone.ft, ...), custom_call_target="tpu_custom_call" | custom-call | tf_op jit(solution)/shard_map/pallas_call | solution.py:458
  86.7 2.5 %copy.9 = bf16[4,16,64,128]{3,2,1,0:T(8,128)(2,1)} copy(bf16[4,16,64,128]{3,1,2,0:T(8,128)(2,1)} %bitcast.3) | data formatting | bytes 2097152 | tf_op jit(solution)/shard_map/transpose | solution.py:449

commit v2 on v1

--- a/solution.py
+++ b/solution.py
@@ -12,6 +12,7 @@
 CONVS = 3
 LON_DEVICES = 16
 LAT_DEVICES = 8
+HALF = 4
 CHIPS = 8
 COLS = 1024
 STRIPS = 16
@@ -63,8 +64,10 @@
 
 def kernel(field, cw, cb, sr, si, ft, iv, tw, out,
            f_v, cw_v, cb_v, sr_v, si_v, ft_v, iv_v, tw_v, T, SW, X, H1, H2, H3, ST, S,
-           PART, DR, RSEND, RRECV, G,
-           in_sem, lon_s, lon_r, lat_s, lat_r, d_s, d_r, rs_s, rs_r, ag_s, ag_r, fw_s, fw_r):
+           PART, DR, RSEND, RRECV, G, HH, GH,
+           in_sem, lon_s, lon_r, lat_s, lat_r, d_s, d_r, rs_s, rs_r, ag_s, ag_r, fw_s, fw_r,
+           h_s, h_r, g_s, g_r, gf_s, gf_r,
+           RX, RH, lend_s, lend_r, relay_s, relay_r):
     d = lax.axis_index("lon")
     lt = lax.axis_index("lat")
     core = lax.rem(d, 2)
@@ -73,6 +76,9 @@
     right = lax.rem(d + 1, LON_DEVICES)
     left = lax.rem(d + LON_DEVICES - 1, LON_DEVICES)
     outer = jnp.where(core == 0, left, right)
+    across = lax.rem(lt + HALF, LAT_DEVICES)
+    wrap = jnp.where(lt < HALF, HALF - 1 - lt, 3 * HALF - 1 - lt)
+    outermost = jnp.logical_or(lax.rem(lt, HALF) == 0, lax.rem(lt, HALF) == HALF - 1)
     has_up = lt > 0
     has_down = lt < LAT_DEVICES - 1
 
@@ -101,6 +107,11 @@
     def _():
         pl.semaphore_signal(barrier, inc=1, device_id={"lat": lt + 1}, device_id_type=MESH)
 
+    @pl.when(outermost)
+    def _():
+        pl.semaphore_signal(barrier, inc=1, device_id={"lat": across}, device_id_type=MESH)
+        pl.semaphore_signal(barrier, inc=1, device_id={"lat": wrap}, device_id_type=MESH)
+
     @pl.when(jnp.logical_not(has_up))
     def _():
         for b in range(BLOCKS):
@@ -111,16 +122,20 @@
         for b in range(BLOCKS):
             X[b, 7:10] = jnp.zeros((3, EXT, STRIPS, CH), BF16)
 
+    def permute(first, last):
+        for row in range(ROWS):
+            for t in range(first, last):
+                X[0, 3 + row, t] = S[row, pl.ds(t - 3, STRIPS, stride=TILES), :].astype(BF16)
+
     with scope("permute_in"):
         loads[0].wait()
         for row in range(ROWS):
             S[row] = f_v[row].astype(F32)
-            for q in range(TILES):
-                X[0, 3 + row, 3 + q] = S[row, pl.ds(q, STRIPS, stride=TILES), :].astype(BF16)
-
+        permute(9, 20)
     with scope("barrier"):
         pl.semaphore_wait(
             barrier, CHIPS + 1 + has_up.astype(jnp.int32) + has_down.astype(jnp.int32)
+            + 2 * outermost.astype(jnp.int32)
         )
 
     def build_weights():
@@ -168,129 +183,371 @@
     strip = lax.broadcasted_iota(jnp.int32, (STRIPS, CH), 0)
     sub = lax.rem(lax.broadcasted_iota(jnp.int32, (ROWS * OWNED, 2 * CH), 0), OWNED)
 
-    def convolve(source, target, index, layer, b, at, to, pairs, masks):
-        bias = cb_v[layer, pl.ds(b, 1), :]
+    def convolve(source, target, b, layer, at, to, step, pairs, masks):
+        bias = cb_v[layer, b:b + 1, :]
         for pair in range(pairs):
             lhs = jnp.concatenate(
-                [source(2 * pair + r, at + tap).reshape(STEP * STRIPS, CH)
+                [source(2 * pair + r, at + tap).reshape(step * STRIPS, CH)
                  for tap in range(3) for r in range(4)], axis=1)
-            total = jnp.dot(lhs, T[index], preferred_element_type=F32)
+            total = jnp.dot(lhs, T[b * CONVS + layer], preferred_element_type=F32)
             for o in range(2):
                 half = 0.5 * (total[:, o * CH:(o + 1) * CH] + bias)
                 value = half * jnp.tanh(half) + half
                 mask = masks.get(2 * pair + o)
                 if mask is not None:
                     value = value * mask
-                target[2 * pair + o, pl.ds(to, STEP)] = value.astype(BF16).reshape(
-                    STEP, STRIPS, CH
+                target[2 * pair + o, pl.ds(to, step)] = value.astype(BF16).reshape(
+                    step, STRIPS, CH
                 )
+
+    def three(b, s1, s2, s3, step):
+        with scope("conv"):
+            convolve(lambda r, t: X[b, r, pl.ds(t, step)], H1, b, 0, s1 - 1, s1, step, 4,
+                     {0: up_mask, 1: up_mask, 6: down_mask, 7: down_mask})
+            convolve(lambda r, t: H1[r, pl.ds(t, step)], H2, b, 1, s2 - 1, s2, step, 3,
+                     {0: up_mask, 5: down_mask})
+            convolve(lambda r, t: H2[r, pl.ds(t, step)], H3.at[b], b, 2, s3 - 1, s3, step, 2, {})
+
+    def lon_pair(b, first, count):
+        rows = pl.ds(first, count)
+        return (
+            pltpu.make_async_remote_copy(
+                src_ref=X.at[b, rows, 64:67], dst_ref=ST.at[b, 0, rows],
+                send_sem=lon_s.at[0], recv_sem=lon_r.at[b, 0],
+                device_id={"lon": right}, device_id_type=MESH),
+            pltpu.make_async_remote_copy(
+                src_ref=X.at[b, rows, 3:6], dst_ref=ST.at[b, 1, rows],
+                send_sem=lon_s.at[1], recv_sem=lon_r.at[b, 1],
+                device_id={"lon": left}, device_id_type=MESH),
+        )
+
+    def lon_halo(b, pair, first, count):
+        with scope("lonwait"):
+            for copy in pair:
+                copy.wait()
+        for row in range(first, first + count):
+            for j in range(3):
+                own = X[b, row, 64 + j].astype(F32)
+                other = ST[b, 0, row, j].astype(F32)
+                tile = jnp.where(strip == 0, pltpu.roll(other, 1, 0), pltpu.roll(own, 1, 0))
+                X[b, row, j] = tile.astype(BF16)
+                own = X[b, row, 3 + j].astype(F32)
+                other = ST[b, 1, row, j].astype(F32)
+                tile = jnp.where(
+                    strip == STRIPS - 1,
+                    pltpu.roll(other, STRIPS - 1, 0), pltpu.roll(own, STRIPS - 1, 0))
+                X[b, row, 67 + j] = tile.astype(BF16)
+
+    def both_ways(down, up):
+        def start(*piece):
+            @pl.when(has_down)
+            def _():
+                down(*piece).start()
+
+            @pl.when(has_up)
+            def _():
+                up(*piece).start()
+
+        def wait_recv(*piece):
+            @pl.when(has_up)
+            def _():
+                down(*piece).wait_recv()
+
+            @pl.when(has_down)
+            def _():
+                up(*piece).wait_recv()
+
+        def wait_send(*piece):
+            @pl.when(has_down)
+            def _():
+                down(*piece).wait_send()
+
+            @pl.when(has_up)
+            def _():
+                up(*piece).wait_send()
+
+        return start, wait_recv, wait_send
+
+    def halo_ways(source, target, buffer, down_row, up_row, other_side, sends, recvs, base):
+        def direct(way, count, first, tiles, slot):
+            at = up_row if way else down_row
+            to = other_side if way else 0
+            window = pl.ds(first, tiles)
+            return pltpu.make_async_remote_copy(
+                src_ref=source.at[pl.ds(at, count), window],
+                dst_ref=target.at[pl.ds(to, count), window],
+                send_sem=sends.at[way, slot], recv_sem=recvs.at[way, slot],
+                device_id={"lat": lt + 1 - 2 * way}, device_id_type=MESH)
+
+        def lend(way, first, tiles, slot):
+            at = (up_row if way else down_row) + 2
+            window = pl.ds(first, tiles)
+            return pltpu.make_async_remote_copy(
+                src_ref=source.at[at, window], dst_ref=buffer.at[window],
+                send_sem=lend_s.at[base + slot], recv_sem=lend_r.at[base + slot],
+                device_id={"lat": across}, device_id_type=MESH)
+
+        def relay(way, first, tiles, slot):
+            to = (other_side if way else 0) + 2
+            window = pl.ds(first, tiles)
+            return pltpu.make_async_remote_copy(
+                src_ref=buffer.at[window], dst_ref=target.at[to, window],
+                send_sem=relay_s.at[base + slot], recv_sem=relay_r.at[base + slot],
+                device_id={"lat": wrap}, device_id_type=MESH)
+
+        def start(*piece):
+            @pl.when(jnp.logical_and(has_down, lt != HALF - 1))
+            def _():
+                direct(0, 3, *piece).start()
+
+            @pl.when(lt == HALF - 1)
+            def _():
+                direct(0, 2, *piece).start()
+                lend(0, *piece).start()
+
+            @pl.when(jnp.logical_and(has_up, lt != HALF))
+            def _():
+                direct(1, 3, *piece).start()
+
+            @pl.when(lt == HALF)
+            def _():
+                direct(1, 2, *piece).start()
+                lend(1, *piece).start()
+
+        def forward(*piece):
+            @pl.when(lt == LAT_DEVICES - 1)
+            def _():
+                lend(0, *piece).wait_recv()
+                relay(0, *piece).start()
+
+            @pl.when(lt == 0)
+            def _():
+                lend(1, *piece).wait_recv()
+                relay(1, *piece).start()
+
+        def wait_recv(*piece):
+            @pl.when(jnp.logical_and(has_up, lt != HALF))
+            def _():
+                direct(0, 3, *piece).wait_recv()
+
+            @pl.when(lt == HALF)
+            def _():
+                direct(0, 2, *piece).wait_recv()
+                relay(0, *piece).wait_recv()
+
+            @pl.when(jnp.logical_and(has_down, lt != HALF - 1))
+            def _():
+                direct(1, 3, *piece).wait_recv()
+
+            @pl.when(lt == HALF - 1)
+            def _():
+                direct(1, 2, *piece).wait_recv()
+                relay(1, *piece).wait_recv()
+
+        def wait_send(*piece):
+            @pl.when(jnp.logical_and(has_down, lt != HALF - 1))
+            def _():
+                direct(0, 3, *piece).wait_send()
+
+            @pl.when(lt == HALF - 1)
+            def _():
+                direct(0, 2, *piece).wait_send()
+                lend(0, *piece).wait_send()
+
+            @pl.when(jnp.logical_and(has_up, lt != HALF))
+            def _():
+                direct(1, 3, *piece).wait_send()
+
+            @pl.when(lt == HALF)
+            def _():
+                direct(1, 2, *piece).wait_send()
+                lend(1, *piece).wait_send()
+
+            @pl.when(lt == LAT_DEVICES - 1)
+            def _():
+                relay(0, *piece).wait_send()
+
+            @pl.when(lt == 0)
+            def _():
+                relay(1, *piece).wait_send()
+
+        return start, forward, wait_recv, wait_send
+
+    def g_down():
+        return pltpu.make_async_remote_copy(
+            src_ref=G.at[0, core, :, :, CH:4 * CH], dst_ref=GH.at[0, core],
+            send_sem=g_s.at[0], recv_sem=g_r.at[0],
+            device_id={"lat": lt + 1}, device_id_type=MESH)
+
+    def g_up():
+        return pltpu.make_async_remote_copy(
+            src_ref=G.at[0, core, :, :, 0:3 * CH], dst_ref=GH.at[1, core],
+            send_sem=g_s.at[1], recv_sem=g_r.at[1],
+            device_id={"lat": lt - 1}, device_id_type=MESH)
+
+    def g_share(side, half):
+        return pltpu.make_async_remote_copy(
+            src_ref=GH.at[side, half], dst_ref=GH.at[side, half],
+            send_sem=gf_s.at[side], recv_sem=gf_r.at[side],
+            device_id={"lon": sibling}, device_id_type=MESH)
+
+    def turned(load):
+        his = []
+        los = []
+        for o in range(2):
+            for ch in range(CHIPS):
+                parts = []
+                for value in load(o, ch):
+                    re = value[0:8]
+                    im = value[8:16]
+                    new_re = re * cos - im * sin
+                    new_im = re * sin + im * cos
+                    if o == 1:
+                        new_re = new_re * flip
+                        new_im = new_im * flip
+                    parts.append(jnp.concatenate([new_re, new_im], axis=0))
+                hi, lo = split2(jnp.concatenate(parts, axis=1))
+                his.append(hi)
+                los.append(lo)
+        hi = jnp.concatenate(his, axis=0)
+        lo = jnp.concatenate(los, axis=0)
+        return jnp.concatenate([hi, hi, lo], axis=0)
+
+    def inverse(c, rhs):
+        table = iv_v[pl.ds(c * 256, 256), :]
+        lhs = jnp.concatenate([table, table[:, 0:256]], axis=1)
+        return jnp.dot(lhs, rhs, preferred_element_type=F32)
 
     def result(c):
         return pltpu.make_async_copy(
             X.at[BLOCKS, 3:7, pl.ds(3 + 16 * c, 16)], out.at[:, pl.ds(16 * c, 16)], in_sem.at[c])
 
-    def block(b, _):
-        to_right = pltpu.make_async_remote_copy(
-            src_ref=X.at[b, 3:7, 64:67], dst_ref=ST.at[b, 0],
-            send_sem=lon_s.at[0], recv_sem=lon_r.at[b, 0],
-            device_id={"lon": right}, device_id_type=MESH)
-        to_left = pltpu.make_async_remote_copy(
-            src_ref=X.at[b, 3:7, 3:6], dst_ref=ST.at[b, 1],
-            send_sem=lon_s.at[1], recv_sem=lon_r.at[b, 1],
-            device_id={"lon": left}, device_id_type=MESH)
-        to_right.start()
-        to_left.start()
-        def down_copy(first, count, slot):
-            return pltpu.make_async_remote_copy(
-                src_ref=X.at[b, 4:7, pl.ds(first, count)],
-                dst_ref=X.at[b, 0:3, pl.ds(first, count)],
-                send_sem=lat_s.at[0, slot], recv_sem=lat_r.at[b, 0, slot],
-                device_id={"lat": lt + 1}, device_id_type=MESH)
-
-        def up_copy(first, count, slot):
-            return pltpu.make_async_remote_copy(
-                src_ref=X.at[b, 3:6, pl.ds(first, count)],
-                dst_ref=X.at[b, 7:10, pl.ds(first, count)],
-                send_sem=lat_s.at[1, slot], recv_sem=lat_r.at[b, 1, slot],
-                device_id={"lat": lt - 1}, device_id_type=MESH)
-
-        pieces = [(17, 19, 0), (36, 17, 1), (53, 17, 2), (0, 17, 3)]
-
-        def start(some):
-            @pl.when(has_down)
-            def _():
-                for piece in some:
-                    down_copy(*piece).start()
-
-            @pl.when(has_up)
-            def _():
-                for piece in some:
-                    up_copy(*piece).start()
-
-        start(pieces[:2])
-        with scope("lonwait"):
-            to_right.wait()
-            to_left.wait()
-        with scope("halo"):
-            for row in range(ROWS):
-                for j in range(3):
-                    own = X[b, 3 + row, 64 + j].astype(F32)
-                    other = ST[b, 0, row, j].astype(F32)
-                    tile = jnp.where(strip == 0, pltpu.roll(other, 1, 0), pltpu.roll(own, 1, 0))
-                    X[b, 3 + row, j] = tile.astype(BF16)
-                    own = X[b, 3 + row, 3 + j].astype(F32)
-                    other = ST[b, 1, row, j].astype(F32)
-                    tile = jnp.where(
-                        strip == STRIPS - 1,
-                        pltpu.roll(other, STRIPS - 1, 0), pltpu.roll(own, STRIPS - 1, 0))
-                    X[b, 3 + row, 67 + j] = tile.astype(BF16)
-        start(pieces[2:])
-
-        @pl.when(b == 0)
-        def _():
-            with scope("build"):
-                build_weights()
-
-        def arrive(first, count, slot):
-            @pl.when(has_up)
-            def _():
-                down_copy(first, count, slot).wait_recv()
-
-            @pl.when(has_down)
-            def _():
-                up_copy(first, count, slot).wait_recv()
+    x_pieces = ([(9, 11, 0)] + [(20 + 9 * k, 9, k + 1) for k in range(5)]
+                + [(65, 5, 6), (0, 9, 7)])
+    h_pieces = [(12, 14, 0), (26, 18, 1), (44, 14, 2), (58, 9, 3), (3, 9, 4)]
+    x_start, x_forward, x_wait, x_done = halo_ways(
+        X.at[0], X.at[0], RX, 4, 3, 7, lat_s, lat_r, 0)
+    h_start, h_forward, h_wait, h_done = halo_ways(
+        H3.at[0], HH, RH, 1, 0, 3, h_s, h_r, 8)
+    g_start, g_wait, g_done = both_ways(g_down, g_up)
+
+    def first_convolutions():
+        x_start(*x_pieces[0])
+        permute(20, 67)
+        for piece in x_pieces[1:6]:
+            x_start(*piece)
+        permute(3, 9)
+        pair = lon_pair(0, 3, 4)
+        for copy in pair:
+            copy.start()
+        lon_halo(0, pair, 3, 4)
+        for piece in x_pieces[6:]:
+            x_start(*piece)
+        with scope("build"):
+            build_weights()
+
+        x_forward(*x_pieces[0])
+        x_forward(*x_pieces[1])
+
+        def chunk(k, _):
+            @pl.when(k < 4)
+            def _():
+                x_forward(29 + 9 * k, 9, k + 2)
+
+            for p in range(6, 8):
+                @pl.when(k == p - 2)
+                def _():
+                    x_forward(*x_pieces[p])
+
+            @pl.when(k == 6)
+            def _():
+                h_forward(*h_pieces[0])
+
+            with scope("latwait"):
+                @pl.when(k == 0)
+                def _():
+                    x_wait(*x_pieces[0])
+
+                @pl.when(jnp.logical_and(k > 0, k < 6))
+                def _():
+                    x_wait(11 + 9 * k, 9, k)
+
+                @pl.when(k == 6)
+                def _():
+                    x_wait(*x_pieces[6])
+
+                @pl.when(k == 7)
+                def _():
+                    x_wait(*x_pieces[7])
+
+            for p in range(3):
+                @pl.when(k == 2 * p + 2)
+                def _():
+                    h_start(*h_pieces[p])
+
+            s1 = jnp.where(k < 6, 10 + 9 * k, jnp.where(k == 6, 60, 1))
+            shift = jnp.where(k == 7, 1, -1)
+            three(0, s1, s1 + shift, s1 + 2 * shift, 9)
+            return 0
+
+        lax.fori_loop(0, 8, chunk, 0)
+
+    def second_convolutions():
+        with scope("gwait"):
+            g_wait()
+            for side, present in ((0, has_up), (1, has_down)):
+                @pl.when(present)
+                def _():
+                    g_share(side, core).start()
+        with scope("hwait"):
+            for piece in h_pieces:
+                h_wait(*piece)
+        with scope("sharewait"):
+            for side, present in ((0, has_up), (1, has_down)):
+                @pl.when(present)
+                def _():
+                    g_share(side, 1 - core).wait_recv()
+        rhs = turned(lambda o, ch: [
+            GH[side, o, ch, :, l * CH:(l + 1) * CH].astype(F32)
+            for side in range(2) for l in range(3)])
+
+        def rows(c, _):
+            spectral = inverse(c, rhs)
+            tiles = pl.ds(3 + 16 * c, 16)
+            for side, present in ((0, has_up), (1, has_down)):
+                @pl.when(present)
+                def _():
+                    for l in range(3):
+                        x = X[0, 7 * side + l, tiles].reshape(256, CH).astype(F32)
+                        h = HH[3 * side + l, tiles].reshape(256, CH).astype(F32)
+                        lanes = slice((3 * side + l) * CH, (3 * side + l + 1) * CH)
+                        value = jnp.tanh(x + h + spectral[:, lanes])
+                        X[1, 7 * side + l, tiles] = value.astype(BF16).reshape(16, STRIPS, CH)
+            return 0
+
+        with scope("halorows"):
+            lax.fori_loop(0, 4, rows, 0)
+        pair = lon_pair(1, 0, 10)
+        for copy in pair:
+            copy.start()
 
         def chunk(c, _):
-            with scope("latwait"):
-                @pl.when(c == 0)
-                def _():
-                    arrive(*pieces[0])
-
-                @pl.when(c > 0)
-                def _():
-                    arrive(jnp.where(c == 3, 0, 19 + STEP * c), STEP, c)
-
-            last = (c == 3).astype(jnp.int32)
+            @pl.when(c == 2)
+            def _():
+                lon_halo(1, pair, 0, 10)
+
             s1 = jnp.where(c == 3, 1, 18 + STEP * c)
-            s2 = s1 - 1 + 2 * last
-            s3 = s1 - 2 + 4 * last
-            with scope("conv1"):
-                convolve(lambda r, t: X[b, r, pl.ds(t, STEP)], H1, b * CONVS, 0, b, s1 - 1, s1, 4,
-                         {0: up_mask, 1: up_mask, 6: down_mask, 7: down_mask})
-            with scope("conv2"):
-                convolve(lambda r, t: H1[r, pl.ds(t, STEP)], H2, b * CONVS + 1, 1, b, s2 - 1, s2, 3,
-                         {0: up_mask, 5: down_mask})
-            with scope("conv3"):
-                convolve(lambda r, t: H2[r, pl.ds(t, STEP)], H3, b * CONVS + 2, 2, b, s3 - 1, s3, 2,
-                         {})
+            shift = jnp.where(c == 3, 1, -1)
+            three(1, s1, s1 + shift, s1 + 2 * shift, STEP)
             return 0
 
         lax.fori_loop(0, 4, chunk, 0)
 
+    def spectral_part(b):
         with scope("dft"):
             for half in range(2):
                 rhs = jnp.concatenate(
-                    [H3[2 * half + l, 3:67].reshape(COLS, CH) for l in range(2)], axis=1)
+                    [H3[b, 2 * half + l, 3:67].reshape(COLS, CH) for l in range(2)], axis=1)
                 both = jnp.dot(ft_v[...], rhs, preferred_element_type=F32)
                 total = both[0:256] + both[256:512]
                 for o in range(2):
@@ -308,6 +565,10 @@
                             PART[o, ch, 0:8, lanes] = new_re
                             PART[o, ch, 8:16, lanes] = new_im
 
+        if b == 0:
+            h_start(*h_pieces[3])
+            h_start(*h_pieces[4])
+            h_forward(*h_pieces[1])
         swap = pltpu.make_async_remote_copy(
             src_ref=PART.at[1 - core], dst_ref=DR.at[b],
             send_sem=d_s.at[0], recv_sem=d_r.at[b],
@@ -333,6 +594,9 @@
         for j in range(1, CHIPS):
             spectrum = spectrum + RRECV[b, j - 1]
 
+        if b == 0:
+            for piece in h_pieces[2:]:
+                h_forward(*piece)
         with scope("mix"):
             lhs = jnp.concatenate(
                 [jnp.concatenate([spectrum[0:8, l * CH:(l + 1) * CH],
@@ -373,6 +637,8 @@
             send_sem=fw_s.at[0], recv_sem=fw_r.at[b],
             device_id={"lon": sibling}, device_id_type=MESH)
         forward.start()
+        if b == 0:
+            g_start()
         back = pltpu.make_async_remote_copy(
             src_ref=G.at[b, 1 - core], dst_ref=G.at[b, 1 - core],
             send_sem=fw_s.at[0], recv_sem=fw_r.at[b],
@@ -380,66 +646,44 @@
         with scope("fwwait"):
             back.wait_recv()
 
-        his = []
-        los = []
-        for o in range(2):
-            for ch in range(CHIPS):
-                parts = []
-                for l in range(ROWS):
-                    value = G[b, o, ch, :, l * CH:(l + 1) * CH].astype(F32)
-                    re = value[0:8]
-                    im = value[8:16]
-                    new_re = re * cos - im * sin
-                    new_im = re * sin + im * cos
-                    if o == 1:
-                        new_re = new_re * flip
-                        new_im = new_im * flip
-                    parts.append(jnp.concatenate([new_re, new_im], axis=0))
-                hi, lo = split2(jnp.concatenate(parts, axis=1))
-                his.append(hi)
-                los.append(lo)
-        hi = jnp.concatenate(his, axis=0)
-        lo = jnp.concatenate(los, axis=0)
-        rhs = jnp.concatenate([hi, hi, lo], axis=0)
+        rhs = turned(lambda o, ch: [
+            G[b, o, ch, :, l * CH:(l + 1) * CH].astype(F32) for l in range(ROWS)])
 
         def finish(c, _):
-            rows = pl.ds(c * 256, 256)
-            table = iv_v[rows, :]
-            lhs = jnp.concatenate([table, table[:, 0:256]], axis=1)
-            spectral = jnp.dot(lhs, rhs, preferred_element_type=F32)
+            spectral = inverse(c, rhs)
             for l in range(ROWS):
                 x = X[b, 3 + l, pl.ds(3 + 16 * c, 16)].reshape(256, CH).astype(F32)
-                h = H3[l, pl.ds(3 + 16 * c, 16)].reshape(256, CH).astype(F32)
+                h = H3[b, l, pl.ds(3 + 16 * c, 16)].reshape(256, CH).astype(F32)
                 value = jnp.tanh(x + h + spectral[:, l * CH:(l + 1) * CH])
                 X[b + 1, 3 + l, pl.ds(3 + 16 * c, 16)] = value.astype(BF16).reshape(
                     16, STRIPS, CH)
 
-            @pl.when(b == BLOCKS - 1)
-            def _():
+            if b == BLOCKS - 1:
                 result(c).start()
 
             return 0
 
         with scope("finish"):
             lax.fori_loop(0, 4, finish, 0)
-
-        @pl.when(has_down)
-        def _():
-            for piece in pieces:
-                down_copy(*piece).wait_send()
-
-        @pl.when(has_up)
-        def _():
-            for piece in pieces:
-                up_copy(*piece).wait_send()
 
         for j in range(1, CHIPS):
             gather(j).wait_send()
         forward.wait_send()
-        return 0
-
-    lax.fori_loop(0, BLOCKS, block, 0)
-
+
+    first_convolutions()
+    spectral_part(0)
+    second_convolutions()
+    spectral_part(1)
+
+    for piece in x_pieces:
+        x_done(*piece)
+    for piece in h_pieces:
+        h_done(*piece)
+    g_done()
+    for side, present in ((0, has_up), (1, has_down)):
+        @pl.when(present)
+        def _():
+            g_share(side, core).wait_send()
     with scope("store"):
         for c in range(4):
             result(c).wait()
@@ -466,19 +710,24 @@
             pltpu.VMEM((BLOCKS + 1, 10, EXT) + tile, BF16),
             pltpu.VMEM((8, EXT) + tile, BF16),
             pltpu.VMEM((6, EXT) + tile, BF16),
-            pltpu.VMEM((4, EXT) + tile, BF16),
-            pltpu.VMEM((BLOCKS, 2, ROWS, 3) + tile, BF16),
+            pltpu.VMEM((BLOCKS, 4, EXT) + tile, BF16),
+            pltpu.VMEM((BLOCKS, 2, 10, 3) + tile, BF16),
             pltpu.VMEM((ROWS, COLS, CH), F32),
             pltpu.VMEM((2, CHIPS, 16, ROWS * CH), F32),
             pltpu.VMEM((BLOCKS, CHIPS, 16, ROWS * CH), F32),
             pltpu.VMEM((CHIPS, 16, ROWS * CH), F32),
             pltpu.VMEM((BLOCKS, CHIPS - 1, 16, ROWS * CH), F32),
             pltpu.VMEM((BLOCKS, 2, CHIPS, 16, ROWS * CH), BF16),
-            dma((8,)), dma((2,)), dma((BLOCKS, 2)), dma((2, 5)), dma((BLOCKS, 2, 5)),
+            pltpu.VMEM((6, EXT) + tile, BF16),
+            pltpu.VMEM((2, 2, CHIPS, 16, 3 * CH), BF16),
+            dma((8,)), dma((2,)), dma((BLOCKS, 2)), dma((2, 8)), dma((2, 8)),
             dma((1,)), dma((BLOCKS,)),
             dma((CHIPS - 1,)), dma((BLOCKS, CHIPS - 1)),
             dma((CHIPS - 1,)), dma((BLOCKS, CHIPS - 1)),
             dma((1,)), dma((BLOCKS,)),
+            dma((2, 5)), dma((2, 5)), dma((2,)), dma((2,)), dma((2,)), dma((2,)),
+            pltpu.VMEM((EXT,) + tile, BF16), pltpu.VMEM((EXT,) + tile, BF16),
+            dma((13,)), dma((13,)), dma((13,)), dma((13,)),
         ],
         compiler_params=pltpu.CompilerParams(
             collective_id=0, has_side_effects=True, vmem_limit_bytes=62 * 1024 * 1024),

time: 89.3 us -> 86.4 us (0.968)
  Pallas kernels: 86.7 us -> 83.8 us
    pallas_call x1, Pallas kernels: 86.7 us -> 83.8 us  [per_device(): pl.pallas_call(kernel, out_shape=jax.ShapeDtypeStruct((ROWS, TILES) + til...]
where the time goes in v2:
time: 86.4 us; the launch traced here: 86.3 us
  Pallas kernels  83.8 us (97%)
  local copies, waits for them, and re-layouts  2.47 us (3%)
    pallas_call x1, Pallas kernels, per_device(): pl.pallas_call(kernel, out_shape=jax.ShapeDtypeStruct((ROWS, TILES) + til...  83.8 us
    transpose x1, local copies, waits for them, and re-layouts, restore(): return jnp.transpose(strips, (0, 2, 1, 3)).reshape(ROWS, COLS, CH)  2.47 us

profile of v2, /device:TPU:25, one launch (start us, length us, event | category | flops | bytes accessed | tf_op | source)
XLA Modules:
  0.0 86.3 jit_solution(18068395782721943568)
XLA Ops:
  0.0 83.8 %shard_map.82 = bf16[4,64,16,128]{3,2,1,0:T(8,128)(2,1)} custom-call(bf16[4,1024,128]{2,1,0:T(8,128)(2,1)} %field.1, bf16[2,3,3,3,128,128]{5,4,3,2,1,0:T(8,128)(2,1)} %cw.1, f32[3,2,128]{2,1,0:T(2,128)} %bitcast.4, bf16[2,8,128,128]{3,2,1,0:T(8,128)(2,1)} %sr.1, bf16[2,8,128,128]{3,2,1,0:T(8,128)(2,1)} %si.1, bf16[512,1024]{1,0:T(8,128)(2,1)} %constant.6.clone.ft, ...), custom_call_target="tpu_custom_call" | custom-call | tf_op jit(solution)/shard_map/pallas_call | solution.py:702
  83.8 2.5 %copy.9 = bf16[4,16,64,128]{3,2,1,0:T(8,128)(2,1)} copy(bf16[4,16,64,128]{3,1,2,0:T(8,128)(2,1)} %bitcast.3) | data formatting | bytes 2097152 | tf_op jit(solution)/shard_map/transpose | solution.py:693

commit v3 on v2

--- a/solution.py
+++ b/solution.py
@@ -208,16 +208,16 @@
                      {0: up_mask, 5: down_mask})
             convolve(lambda r, t: H2[r, pl.ds(t, step)], H3.at[b], b, 2, s3 - 1, s3, step, 2, {})
 
-    def lon_pair(b, first, count):
+    def lon_pair(b, first, count, slot):
         rows = pl.ds(first, count)
         return (
             pltpu.make_async_remote_copy(
                 src_ref=X.at[b, rows, 64:67], dst_ref=ST.at[b, 0, rows],
-                send_sem=lon_s.at[0], recv_sem=lon_r.at[b, 0],
+                send_sem=lon_s.at[slot, 0], recv_sem=lon_r.at[slot, 0],
                 device_id={"lon": right}, device_id_type=MESH),
             pltpu.make_async_remote_copy(
                 src_ref=X.at[b, rows, 3:6], dst_ref=ST.at[b, 1, rows],
-                send_sem=lon_s.at[1], recv_sem=lon_r.at[b, 1],
+                send_sem=lon_s.at[slot, 1], recv_sem=lon_r.at[slot, 1],
                 device_id={"lon": left}, device_id_type=MESH),
         )
 
@@ -268,7 +268,7 @@
 
         return start, wait_recv, wait_send
 
-    def halo_ways(source, target, buffer, down_row, up_row, other_side, sends, recvs, base):
+    def halo_ways(source, target, buffer, down_row, up_row, other_side, sends, recvs, base, skip):
         def direct(way, count, first, tiles, slot):
             at = up_row if way else down_row
             to = other_side if way else 0
@@ -295,24 +295,26 @@
                 send_sem=relay_s.at[base + slot], recv_sem=relay_r.at[base + slot],
                 device_id={"lat": wrap}, device_id_type=MESH)
 
+        def plain(piece):
+            return isinstance(piece[2], int) and piece[2] < skip
+
+        def each(piece, down, down_split, up, up_split):
+            if plain(piece):
+                pl.when(has_down)(down)
+                pl.when(has_up)(up)
+                return
+            pl.when(jnp.logical_and(has_down, lt != HALF - 1))(down)
+            pl.when(lt == HALF - 1)(down_split)
+            pl.when(jnp.logical_and(has_up, lt != HALF))(up)
+            pl.when(lt == HALF)(up_split)
+
         def start(*piece):
-            @pl.when(jnp.logical_and(has_down, lt != HALF - 1))
-            def _():
-                direct(0, 3, *piece).start()
-
-            @pl.when(lt == HALF - 1)
-            def _():
-                direct(0, 2, *piece).start()
-                lend(0, *piece).start()
-
-            @pl.when(jnp.logical_and(has_up, lt != HALF))
-            def _():
-                direct(1, 3, *piece).start()
-
-            @pl.when(lt == HALF)
-            def _():
-                direct(1, 2, *piece).start()
-                lend(1, *piece).start()
+            def split(way):
+                direct(way, 2, *piece).start()
+                lend(way, *piece).start()
+
+            each(piece, lambda: direct(0, 3, *piece).start(), lambda: split(0),
+                 lambda: direct(1, 3, *piece).start(), lambda: split(1))
 
         def forward(*piece):
             @pl.when(lt == LAT_DEVICES - 1)
@@ -326,50 +328,28 @@
                 relay(1, *piece).start()
 
         def wait_recv(*piece):
-            @pl.when(jnp.logical_and(has_up, lt != HALF))
-            def _():
-                direct(0, 3, *piece).wait_recv()
-
-            @pl.when(lt == HALF)
-            def _():
-                direct(0, 2, *piece).wait_recv()
-                relay(0, *piece).wait_recv()
-
-            @pl.when(jnp.logical_and(has_down, lt != HALF - 1))
-            def _():
-                direct(1, 3, *piece).wait_recv()
-
-            @pl.when(lt == HALF - 1)
-            def _():
-                direct(1, 2, *piece).wait_recv()
-                relay(1, *piece).wait_recv()
+            def split(way):
+                direct(way, 2, *piece).wait_recv()
+                relay(way, *piece).wait_recv()
+
+            each(piece, lambda: direct(1, 3, *piece).wait_recv(), lambda: split(1),
+                 lambda: direct(0, 3, *piece).wait_recv(), lambda: split(0))
 
         def wait_send(*piece):
-            @pl.when(jnp.logical_and(has_down, lt != HALF - 1))
-            def _():
-                direct(0, 3, *piece).wait_send()
-
-            @pl.when(lt == HALF - 1)
-            def _():
-                direct(0, 2, *piece).wait_send()
-                lend(0, *piece).wait_send()
-
-            @pl.when(jnp.logical_and(has_up, lt != HALF))
-            def _():
-                direct(1, 3, *piece).wait_send()
-
-            @pl.when(lt == HALF)
-            def _():
-                direct(1, 2, *piece).wait_send()
-                lend(1, *piece).wait_send()
-
-            @pl.when(lt == LAT_DEVICES - 1)
-            def _():
-                relay(0, *piece).wait_send()
-
-            @pl.when(lt == 0)
-            def _():
-                relay(1, *piece).wait_send()
+            def split(way):
+                direct(way, 2, *piece).wait_send()
+                lend(way, *piece).wait_send()
+
+            each(piece, lambda: direct(0, 3, *piece).wait_send(), lambda: split(0),
+                 lambda: direct(1, 3, *piece).wait_send(), lambda: split(1))
+            if not plain(piece):
+                @pl.when(lt == LAT_DEVICES - 1)
+                def _():
+                    relay(0, *piece).wait_send()
+
+                @pl.when(lt == 0)
+                def _():
+                    relay(1, *piece).wait_send()
 
         return start, forward, wait_recv, wait_send
 
@@ -426,9 +406,9 @@
                 + [(65, 5, 6), (0, 9, 7)])
     h_pieces = [(12, 14, 0), (26, 18, 1), (44, 14, 2), (58, 9, 3), (3, 9, 4)]
     x_start, x_forward, x_wait, x_done = halo_ways(
-        X.at[0], X.at[0], RX, 4, 3, 7, lat_s, lat_r, 0)
+        X.at[0], X.at[0], RX, 4, 3, 7, lat_s, lat_r, 0, 2)
     h_start, h_forward, h_wait, h_done = halo_ways(
-        H3.at[0], HH, RH, 1, 0, 3, h_s, h_r, 8)
+        H3.at[0], HH, RH, 1, 0, 3, h_s, h_r, 8, 0)
     g_start, g_wait, g_done = both_ways(g_down, g_up)
 
     def first_convolutions():
@@ -437,7 +417,7 @@
         for piece in x_pieces[1:6]:
             x_start(*piece)
         permute(3, 9)
-        pair = lon_pair(0, 3, 4)
+        pair = lon_pair(0, 3, 4, 0)
         for copy in pair:
             copy.start()
         lon_halo(0, pair, 3, 4)
@@ -446,9 +426,6 @@
         with scope("build"):
             build_weights()
 
-        x_forward(*x_pieces[0])
-        x_forward(*x_pieces[1])
-
         def chunk(k, _):
             @pl.when(k < 4)
             def _():
@@ -468,7 +445,11 @@
                 def _():
                     x_wait(*x_pieces[0])
 
-                @pl.when(jnp.logical_and(k > 0, k < 6))
+                @pl.when(k == 1)
+                def _():
+                    x_wait(*x_pieces[1])
+
+                @pl.when(jnp.logical_and(k > 1, k < 6))
                 def _():
                     x_wait(11 + 9 * k, 9, k)
 
@@ -493,6 +474,9 @@
         lax.fori_loop(0, 8, chunk, 0)
 
     def second_convolutions():
+        own = lon_pair(1, 3, 4, 1)
+        for copy in own:
+            copy.start()
         with scope("gwait"):
             g_wait()
             for side, present in ((0, has_up), (1, has_down)):
@@ -527,14 +511,17 @@
 
         with scope("halorows"):
             lax.fori_loop(0, 4, rows, 0)
-        pair = lon_pair(1, 0, 10)
-        for copy in pair:
+        top = lon_pair(1, 0, 3, 2)
+        bottom = lon_pair(1, 7, 3, 3)
+        for copy in top + bottom:
             copy.start()
 
         def chunk(c, _):
             @pl.when(c == 2)
             def _():
-                lon_halo(1, pair, 0, 10)
+                lon_halo(1, own, 3, 4)
+                lon_halo(1, top, 0, 3)
+                lon_halo(1, bottom, 7, 3)
 
             s1 = jnp.where(c == 3, 1, 18 + STEP * c)
             shift = jnp.where(c == 3, 1, -1)
@@ -588,6 +575,16 @@
         for j in range(1, CHIPS):
             scatter(j).start()
         spectrum = RSEND[chip]
+        if b == 1:
+            for piece in x_pieces:
+                x_done(*piece)
+            for piece in h_pieces:
+                h_done(*piece)
+            g_done()
+            for side, present in ((0, has_up), (1, has_down)):
+                @pl.when(present)
+                def _():
+                    g_share(side, core).wait_send()
         with scope("rswait"):
             for j in range(1, CHIPS):
                 scatter(j).wait()
@@ -675,15 +672,6 @@
     second_convolutions()
     spectral_part(1)
 
-    for piece in x_pieces:
-        x_done(*piece)
-    for piece in h_pieces:
-        h_done(*piece)
-    g_done()
-    for side, present in ((0, has_up), (1, has_down)):
-        @pl.when(present)
-        def _():
-            g_share(side, core).wait_send()
     with scope("store"):
         for c in range(4):
             result(c).wait()
@@ -720,7 +708,7 @@
             pltpu.VMEM((BLOCKS, 2, CHIPS, 16, ROWS * CH), BF16),
             pltpu.VMEM((6, EXT) + tile, BF16),
             pltpu.VMEM((2, 2, CHIPS, 16, 3 * CH), BF16),
-            dma((8,)), dma((2,)), dma((BLOCKS, 2)), dma((2, 8)), dma((2, 8)),
+            dma((8,)), dma((4, 2)), dma((4, 2)), dma((2, 8)), dma((2, 8)),
             dma((1,)), dma((BLOCKS,)),
             dma((CHIPS - 1,)), dma((BLOCKS, CHIPS - 1)),
             dma((CHIPS - 1,)), dma((BLOCKS, CHIPS - 1)),

time: 86.4 us -> 83 us (0.961)
  Pallas kernels: 83.8 us -> 80.3 us
    pallas_call x1, Pallas kernels: 83.8 us -> 80.3 us  [per_device(): pl.pallas_call(kernel, out_shape=jax.ShapeDtypeStruct((ROWS, TILES) + til...]
where the time goes in v3:
time: 83 us; the launch traced here: 82.8 us
  Pallas kernels  80.3 us (97%)
  local copies, waits for them, and re-layouts  2.47 us (3%)
    pallas_call x1, Pallas kernels, per_device(): pl.pallas_call(kernel, out_shape=jax.ShapeDtypeStruct((ROWS, TILES) + til...  80.3 us
    transpose x1, local copies, waits for them, and re-layouts, restore(): return jnp.transpose(strips, (0, 2, 1, 3)).reshape(ROWS, COLS, CH)  2.47 us

profile of v3, /device:TPU:25, one launch (start us, length us, event | category | flops | bytes accessed | tf_op | source)
XLA Modules:
  0.0 82.8 jit_solution(16176682078632076790)
XLA Ops:
  0.0 80.3 %shard_map.82 = bf16[4,64,16,128]{3,2,1,0:T(8,128)(2,1)} custom-call(bf16[4,1024,128]{2,1,0:T(8,128)(2,1)} %field.1, bf16[2,3,3,3,128,128]{5,4,3,2,1,0:T(8,128)(2,1)} %cw.1, f32[3,2,128]{2,1,0:T(2,128)} %bitcast.4, bf16[2,8,128,128]{3,2,1,0:T(8,128)(2,1)} %sr.1, bf16[2,8,128,128]{3,2,1,0:T(8,128)(2,1)} %si.1, bf16[512,1024]{1,0:T(8,128)(2,1)} %constant.6.clone.ft, ...), custom_call_target="tpu_custom_call" | custom-call | tf_op jit(solution)/shard_map/pallas_call | solution.py:690
  80.3 2.5 %copy.9 = bf16[4,16,64,128]{3,2,1,0:T(8,128)(2,1)} copy(bf16[4,16,64,128]{3,1,2,0:T(8,128)(2,1)} %bitcast.3) | data formatting | bytes 2097152 | tf_op jit(solution)/shard_map/transpose | solution.py:681

commit v4 on v3

--- a/solution.py
+++ b/solution.py
@@ -22,6 +22,7 @@
 OWNED = 8
 EXT = 70
 STEP = 17
+PEERS = ((1, 2), (0, 2), (1, 1), (1, 3), (0, 1), (0, 3), (1, 0))
 F32 = jnp.float32
 BF16 = jnp.bfloat16
 MESH = pl.DeviceIdType.MESH
@@ -67,7 +68,7 @@
            PART, DR, RSEND, RRECV, G, HH, GH,
            in_sem, lon_s, lon_r, lat_s, lat_r, d_s, d_r, rs_s, rs_r, ag_s, ag_r, fw_s, fw_r,
            h_s, h_r, g_s, g_r, gf_s, gf_r,
-           RX, RH, lend_s, lend_r, relay_s, relay_r):
+           RX, RH, edge_s, edge_r):
     d = lax.axis_index("lon")
     lt = lax.axis_index("lat")
     core = lax.rem(d, 2)
@@ -95,9 +96,14 @@
     barrier = pltpu.get_barrier_semaphore()
     pl.semaphore_signal(barrier, inc=1, device_id={"lon": sibling}, device_id_type=MESH)
     pl.semaphore_signal(barrier, inc=1, device_id={"lon": outer}, device_id_type=MESH)
-    for j in range(1, CHIPS):
-        peer = lax.rem(chip + j, CHIPS) * 2 + core
-        pl.semaphore_signal(barrier, inc=1, device_id={"lon": peer}, device_id_type=MESH)
+
+    def peer_at(dz, dx):
+        z = lax.div(chip, 4)
+        return (1 - z if dz else z) * 4 + lax.rem(chip + dx, 4)
+
+    for where in PEERS:
+        pl.semaphore_signal(
+            barrier, inc=1, device_id={"lon": peer_at(*where) * 2 + core}, device_id_type=MESH)
 
     @pl.when(has_up)
     def _():
@@ -183,11 +189,14 @@
     strip = lax.broadcasted_iota(jnp.int32, (STRIPS, CH), 0)
     sub = lax.rem(lax.broadcasted_iota(jnp.int32, (ROWS * OWNED, 2 * CH), 0), OWNED)
 
-    def convolve(source, target, b, layer, at, to, step, pairs, masks):
+    def convolve(source, target, b, layer, starts, step, pairs, masks):
         bias = cb_v[layer, b:b + 1, :]
+        size = step * STRIPS
         for pair in range(pairs):
             lhs = jnp.concatenate(
-                [source(2 * pair + r, at + tap).reshape(step * STRIPS, CH)
+                [jnp.concatenate(
+                    [source(2 * pair + r, start - 1 + tap).reshape(size, CH)
+                     for start in starts], axis=0)
                  for tap in range(3) for r in range(4)], axis=1)
             total = jnp.dot(lhs, T[b * CONVS + layer], preferred_element_type=F32)
             for o in range(2):
@@ -196,17 +205,18 @@
                 mask = masks.get(2 * pair + o)
                 if mask is not None:
                     value = value * mask
-                target[2 * pair + o, pl.ds(to, step)] = value.astype(BF16).reshape(
-                    step, STRIPS, CH
-                )
+                value = value.astype(BF16)
+                for i, start in enumerate(starts):
+                    target[2 * pair + o, pl.ds(start, step)] = value[
+                        i * size:(i + 1) * size].reshape(step, STRIPS, CH)
 
     def three(b, s1, s2, s3, step):
         with scope("conv"):
-            convolve(lambda r, t: X[b, r, pl.ds(t, step)], H1, b, 0, s1 - 1, s1, step, 4,
+            convolve(lambda r, t: X[b, r, pl.ds(t, step)], H1, b, 0, s1, step, 4,
                      {0: up_mask, 1: up_mask, 6: down_mask, 7: down_mask})
-            convolve(lambda r, t: H1[r, pl.ds(t, step)], H2, b, 1, s2 - 1, s2, step, 3,
+            convolve(lambda r, t: H1[r, pl.ds(t, step)], H2, b, 1, s2, step, 3,
                      {0: up_mask, 5: down_mask})
-            convolve(lambda r, t: H2[r, pl.ds(t, step)], H3.at[b], b, 2, s3 - 1, s3, step, 2, {})
+            convolve(lambda r, t: H2[r, pl.ds(t, step)], H3.at[b], b, 2, s3, step, 2, {})
 
     def lon_pair(b, first, count, slot):
         rows = pl.ds(first, count)
@@ -284,7 +294,7 @@
             window = pl.ds(first, tiles)
             return pltpu.make_async_remote_copy(
                 src_ref=source.at[at, window], dst_ref=buffer.at[window],
-                send_sem=lend_s.at[base + slot], recv_sem=lend_r.at[base + slot],
+                send_sem=edge_s.at[base + slot], recv_sem=edge_r.at[base + slot],
                 device_id={"lat": across}, device_id_type=MESH)
 
         def relay(way, first, tiles, slot):
@@ -292,7 +302,7 @@
             window = pl.ds(first, tiles)
             return pltpu.make_async_remote_copy(
                 src_ref=buffer.at[window], dst_ref=target.at[to, window],
-                send_sem=relay_s.at[base + slot], recv_sem=relay_r.at[base + slot],
+                send_sem=edge_s.at[base + slot], recv_sem=edge_r.at[base + slot],
                 device_id={"lat": wrap}, device_id_type=MESH)
 
         def plain(piece):
@@ -394,21 +404,21 @@
         return jnp.concatenate([hi, hi, lo], axis=0)
 
     def inverse(c, rhs):
-        table = iv_v[pl.ds(c * 256, 256), :]
+        table = iv_v[pl.ds(c * 512, 512), :]
         lhs = jnp.concatenate([table, table[:, 0:256]], axis=1)
         return jnp.dot(lhs, rhs, preferred_element_type=F32)
 
     def result(c):
         return pltpu.make_async_copy(
-            X.at[BLOCKS, 3:7, pl.ds(3 + 16 * c, 16)], out.at[:, pl.ds(16 * c, 16)], in_sem.at[c])
+            X.at[BLOCKS, 3:7, pl.ds(3 + 32 * c, 32)], out.at[:, pl.ds(32 * c, 32)], in_sem.at[c])
 
     x_pieces = ([(9, 11, 0)] + [(20 + 9 * k, 9, k + 1) for k in range(5)]
                 + [(65, 5, 6), (0, 9, 7)])
     h_pieces = [(12, 14, 0), (26, 18, 1), (44, 14, 2), (58, 9, 3), (3, 9, 4)]
     x_start, x_forward, x_wait, x_done = halo_ways(
-        X.at[0], X.at[0], RX, 4, 3, 7, lat_s, lat_r, 0, 2)
+        X.at[0], X.at[0], RX, 4, 3, 7, lat_s, lat_r, -2, 2)
     h_start, h_forward, h_wait, h_done = halo_ways(
-        H3.at[0], HH, RH, 1, 0, 3, h_s, h_r, 8, 0)
+        H3.at[0], HH, RH, 1, 0, 3, h_s, h_r, 6, 0)
     g_start, g_wait, g_done = both_ways(g_down, g_up)
 
     def first_convolutions():
@@ -468,7 +478,7 @@
 
             s1 = jnp.where(k < 6, 10 + 9 * k, jnp.where(k == 6, 60, 1))
             shift = jnp.where(k == 7, 1, -1)
-            three(0, s1, s1 + shift, s1 + 2 * shift, 9)
+            three(0, [s1], [s1 + shift], [s1 + 2 * shift], 9)
             return 0
 
         lax.fori_loop(0, 8, chunk, 0)
@@ -497,38 +507,40 @@
 
         def rows(c, _):
             spectral = inverse(c, rhs)
-            tiles = pl.ds(3 + 16 * c, 16)
+            tiles = pl.ds(3 + 32 * c, 32)
             for side, present in ((0, has_up), (1, has_down)):
                 @pl.when(present)
                 def _():
                     for l in range(3):
-                        x = X[0, 7 * side + l, tiles].reshape(256, CH).astype(F32)
-                        h = HH[3 * side + l, tiles].reshape(256, CH).astype(F32)
+                        x = X[0, 7 * side + l, tiles].reshape(512, CH).astype(F32)
+                        h = HH[3 * side + l, tiles].reshape(512, CH).astype(F32)
                         lanes = slice((3 * side + l) * CH, (3 * side + l + 1) * CH)
                         value = jnp.tanh(x + h + spectral[:, lanes])
-                        X[1, 7 * side + l, tiles] = value.astype(BF16).reshape(16, STRIPS, CH)
+                        X[1, 7 * side + l, tiles] = value.astype(BF16).reshape(32, STRIPS, CH)
             return 0
 
         with scope("halorows"):
-            lax.fori_loop(0, 4, rows, 0)
+            lax.fori_loop(0, 2, rows, 0)
         top = lon_pair(1, 0, 3, 2)
         bottom = lon_pair(1, 7, 3, 3)
         for copy in top + bottom:
             copy.start()
 
         def chunk(c, _):
-            @pl.when(c == 2)
+            @pl.when(c == 1)
             def _():
                 lon_halo(1, own, 3, 4)
                 lon_halo(1, top, 0, 3)
                 lon_halo(1, bottom, 7, 3)
 
-            s1 = jnp.where(c == 3, 1, 18 + STEP * c)
-            shift = jnp.where(c == 3, 1, -1)
-            three(1, s1, s1 + shift, s1 + 2 * shift, STEP)
+            first = 18 + 34 * c
+            second = 35 - 34 * c
+            shift = 2 * c - 1
+            three(1, [first, second], [first - 1, second + shift],
+                  [first - 2, second + 2 * shift], STEP)
             return 0
 
-        lax.fori_loop(0, 4, chunk, 0)
+        lax.fori_loop(0, 2, chunk, 0)
 
     def spectral_part(b):
         with scope("dft"):
@@ -565,15 +577,15 @@
             swap.wait()
         RSEND[...] = PART[core] + DR[b]
 
-        def scatter(j):
-            peer = lax.rem(chip + j, CHIPS)
+        def scatter(dz, dx):
+            peer = peer_at(dz, dx)
             return pltpu.make_async_remote_copy(
-                src_ref=RSEND.at[peer], dst_ref=RRECV.at[b, j - 1],
-                send_sem=rs_s.at[j - 1], recv_sem=rs_r.at[b, j - 1],
+                src_ref=RSEND.at[peer], dst_ref=RRECV.at[b, 4 * dz + dx - 1],
+                send_sem=rs_s.at[0], recv_sem=rs_r.at[b],
                 device_id={"lon": peer * 2 + core}, device_id_type=MESH)
 
-        for j in range(1, CHIPS):
-            scatter(j).start()
+        for where in PEERS:
+            scatter(*where).start()
         spectrum = RSEND[chip]
         if b == 1:
             for piece in x_pieces:
@@ -586,8 +598,10 @@
                 def _():
                     g_share(side, core).wait_send()
         with scope("rswait"):
-            for j in range(1, CHIPS):
-                scatter(j).wait()
+            pltpu.make_async_remote_copy(
+                src_ref=RSEND.at[0:CHIPS - 1], dst_ref=RRECV.at[b],
+                send_sem=rs_s.at[0], recv_sem=rs_r.at[b],
+                device_id={"lon": sibling}, device_id_type=MESH).wait()
         for j in range(1, CHIPS):
             spectrum = spectrum + RRECV[b, j - 1]
 
@@ -609,26 +623,21 @@
                     [mixed[8 * l:8 * l + 8, 0:CH], mixed[8 * l:8 * l + 8, CH:2 * CH]], axis=0
                 ).astype(BF16)
 
-        def gather(j):
-            peer = lax.rem(chip + j, CHIPS)
+        def gather(dz, dx):
             return pltpu.make_async_remote_copy(
                 src_ref=G.at[b, core, chip], dst_ref=G.at[b, core, chip],
-                send_sem=ag_s.at[j - 1], recv_sem=ag_r.at[b, j - 1],
-                device_id={"lon": peer * 2 + core}, device_id_type=MESH)
-
-        for j in range(1, CHIPS):
-            gather(j).start()
-
-        def arrived(j):
-            peer = lax.rem(chip + CHIPS - j, CHIPS)
-            return pltpu.make_async_remote_copy(
-                src_ref=G.at[b, core, peer], dst_ref=G.at[b, core, peer],
-                send_sem=ag_s.at[j - 1], recv_sem=ag_r.at[b, j - 1],
-                device_id={"lon": peer * 2 + core}, device_id_type=MESH)
-
+                send_sem=ag_s.at[0], recv_sem=ag_r.at[b],
+                device_id={"lon": peer_at(dz, dx) * 2 + core}, device_id_type=MESH)
+
+        for where in PEERS:
+            gather(*where).start()
+
+        gathered = pltpu.make_async_remote_copy(
+            src_ref=G.at[b, core, 0:CHIPS - 1], dst_ref=G.at[b, core, 0:CHIPS - 1],
+            send_sem=ag_s.at[0], recv_sem=ag_r.at[b],
+            device_id={"lon": sibling}, device_id_type=MESH)
         with scope("agwait"):
-            for j in range(1, CHIPS):
-                arrived(j).wait_recv()
+            gathered.wait_recv()
         forward = pltpu.make_async_remote_copy(
             src_ref=G.at[b, core], dst_ref=G.at[b, core],
             send_sem=fw_s.at[0], recv_sem=fw_r.at[b],
@@ -649,11 +658,11 @@
         def finish(c, _):
             spectral = inverse(c, rhs)
             for l in range(ROWS):
-                x = X[b, 3 + l, pl.ds(3 + 16 * c, 16)].reshape(256, CH).astype(F32)
-                h = H3[b, l, pl.ds(3 + 16 * c, 16)].reshape(256, CH).astype(F32)
+                x = X[b, 3 + l, pl.ds(3 + 32 * c, 32)].reshape(512, CH).astype(F32)
+                h = H3[b, l, pl.ds(3 + 32 * c, 32)].reshape(512, CH).astype(F32)
                 value = jnp.tanh(x + h + spectral[:, l * CH:(l + 1) * CH])
-                X[b + 1, 3 + l, pl.ds(3 + 16 * c, 16)] = value.astype(BF16).reshape(
-                    16, STRIPS, CH)
+                X[b + 1, 3 + l, pl.ds(3 + 32 * c, 32)] = value.astype(BF16).reshape(
+                    32, STRIPS, CH)
 
             if b == BLOCKS - 1:
                 result(c).start()
@@ -661,10 +670,9 @@
             return 0
 
         with scope("finish"):
-            lax.fori_loop(0, 4, finish, 0)
-
-        for j in range(1, CHIPS):
-            gather(j).wait_send()
+            lax.fori_loop(0, 2, finish, 0)
+
+        gathered.wait_send()
         forward.wait_send()
 
     first_convolutions()
@@ -673,7 +681,7 @@
     spectral_part(1)
 
     with scope("store"):
-        for c in range(4):
+        for c in range(2):
             result(c).wait()
 
 
@@ -710,12 +718,11 @@
             pltpu.VMEM((2, 2, CHIPS, 16, 3 * CH), BF16),
             dma((8,)), dma((4, 2)), dma((4, 2)), dma((2, 8)), dma((2, 8)),
             dma((1,)), dma((BLOCKS,)),
-            dma((CHIPS - 1,)), dma((BLOCKS, CHIPS - 1)),
-            dma((CHIPS - 1,)), dma((BLOCKS, CHIPS - 1)),
+            dma((1,)), dma((BLOCKS,)), dma((1,)), dma((BLOCKS,)),
             dma((1,)), dma((BLOCKS,)),
             dma((2, 5)), dma((2, 5)), dma((2,)), dma((2,)), dma((2,)), dma((2,)),
             pltpu.VMEM((EXT,) + tile, BF16), pltpu.VMEM((EXT,) + tile, BF16),
-            dma((13,)), dma((13,)), dma((13,)), dma((13,)),
+            dma((11,)), dma((11,)),
         ],
         compiler_params=pltpu.CompilerParams(
             collective_id=0, has_side_effects=True, vmem_limit_bytes=62 * 1024 * 1024),

time: 83 us -> 80.4 us (0.969)
  Pallas kernels: 80.3 us -> 77.8 us
    pallas_call x1, Pallas kernels: 80.3 us -> 77.8 us  [per_device(): pl.pallas_call(kernel, out_shape=jax.ShapeDtypeStruct((ROWS, TILES) + til...]
where the time goes in v4:
time: 80.4 us; the launch traced here: 80.3 us
  Pallas kernels  77.8 us (97%)
  local copies, waits for them, and re-layouts  2.47 us (3%)
    pallas_call x1, Pallas kernels, per_device(): pl.pallas_call(kernel, out_shape=jax.ShapeDtypeStruct((ROWS, TILES) + til...  77.8 us
    transpose x1, local copies, waits for them, and re-layouts, restore(): return jnp.transpose(strips, (0, 2, 1, 3)).reshape(ROWS, COLS, CH)  2.47 us

profile of v4, /device:TPU:25, one launch (start us, length us, event | category | flops | bytes accessed | tf_op | source)
XLA Modules:
  0.0 80.3 jit_solution(11106013843678828922)
XLA Ops:
  0.0 77.8 %shard_map.82 = bf16[4,64,16,128]{3,2,1,0:T(8,128)(2,1)} custom-call(bf16[4,1024,128]{2,1,0:T(8,128)(2,1)} %field.1, bf16[2,3,3,3,128,128]{5,4,3,2,1,0:T(8,128)(2,1)} %cw.1, f32[3,2,128]{2,1,0:T(2,128)} %bitcast.4, bf16[2,8,128,128]{3,2,1,0:T(8,128)(2,1)} %sr.1, bf16[2,8,128,128]{3,2,1,0:T(8,128)(2,1)} %si.1, bf16[512,1024]{1,0:T(8,128)(2,1)} %constant.6.clone.ft, ...), custom_call_target="tpu_custom_call" | custom-call | tf_op jit(solution)/shard_map/pallas_call | solution.py:698
  77.8 2.5 %copy.9 = bf16[4,16,64,128]{3,2,1,0:T(8,128)(2,1)} copy(bf16[4,16,64,128]{3,1,2,0:T(8,128)(2,1)} %bitcast.3) | data formatting | bytes 2097152 | tf_op jit(solution)/shard_map/transpose | solution.py:689

commit v5 on v4

--- a/solution.py
+++ b/solution.py
@@ -90,9 +90,6 @@
              (iv, iv_v), (tw, tw_v)]
         )
     ]
-    for load in loads:
-        load.start()
-
     barrier = pltpu.get_barrier_semaphore()
     pl.semaphore_signal(barrier, inc=1, device_id={"lon": sibling}, device_id_type=MESH)
     pl.semaphore_signal(barrier, inc=1, device_id={"lon": outer}, device_id_type=MESH)
@@ -117,6 +114,9 @@
     def _():
         pl.semaphore_signal(barrier, inc=1, device_id={"lat": across}, device_id_type=MESH)
         pl.semaphore_signal(barrier, inc=1, device_id={"lat": wrap}, device_id_type=MESH)
+
+    for load in loads:
+        load.start()
 
     @pl.when(jnp.logical_not(has_up))
     def _():
@@ -408,9 +408,10 @@
         lhs = jnp.concatenate([table, table[:, 0:256]], axis=1)
         return jnp.dot(lhs, rhs, preferred_element_type=F32)
 
-    def result(c):
+    def result(c, l):
         return pltpu.make_async_copy(
-            X.at[BLOCKS, 3:7, pl.ds(3 + 32 * c, 32)], out.at[:, pl.ds(32 * c, 32)], in_sem.at[c])
+            X.at[BLOCKS, 3 + l, pl.ds(3 + 32 * c, 32)], out.at[l, pl.ds(32 * c, 32)],
+            in_sem.at[4 * c + l])
 
     x_pieces = ([(9, 11, 0)] + [(20 + 9 * k, 9, k + 1) for k in range(5)]
                 + [(65, 5, 6), (0, 9, 7)])
@@ -663,9 +664,9 @@
                 value = jnp.tanh(x + h + spectral[:, l * CH:(l + 1) * CH])
                 X[b + 1, 3 + l, pl.ds(3 + 32 * c, 32)] = value.astype(BF16).reshape(
                     32, STRIPS, CH)
-
-            if b == BLOCKS - 1:
-                result(c).start()
+                if b == BLOCKS - 1:
+                    result(c, l).start()
+
 
             return 0
 
@@ -682,7 +683,8 @@
 
     with scope("store"):
         for c in range(2):
-            result(c).wait()
+            for l in range(ROWS):
+                result(c, l).wait()
 
 
 def restore(strips):

time: 80.4 us -> 80.3 us (level)
  no operation moved by 1% of the time
where the time goes in v5:
time: 80.3 us; the launch traced here: 80.2 us
  Pallas kernels  77.7 us (97%)
  local copies, waits for them, and re-layouts  2.47 us (3%)
    pallas_call x1, Pallas kernels, per_device(): pl.pallas_call(kernel, out_shape=jax.ShapeDtypeStruct((ROWS, TILES) + til...  77.7 us
    transpose x1, local copies, waits for them, and re-layouts, restore(): return jnp.transpose(strips, (0, 2, 1, 3)).reshape(ROWS, COLS, CH)  2.47 us

profile of v5, /device:TPU:25, one launch (start us, length us, event | category | flops | bytes accessed | tf_op | source)
XLA Modules:
  0.0 80.2 jit_solution(16989259794187283451)
XLA Ops:
  0.0 77.7 %shard_map.82 = bf16[4,64,16,128]{3,2,1,0:T(8,128)(2,1)} custom-call(bf16[4,1024,128]{2,1,0:T(8,128)(2,1)} %field.1, bf16[2,3,3,3,128,128]{5,4,3,2,1,0:T(8,128)(2,1)} %cw.1, f32[3,2,128]{2,1,0:T(2,128)} %bitcast.4, bf16[2,8,128,128]{3,2,1,0:T(8,128)(2,1)} %sr.1, bf16[2,8,128,128]{3,2,1,0:T(8,128)(2,1)} %si.1, bf16[512,1024]{1,0:T(8,128)(2,1)} %constant.6.clone.ft, ...), custom_call_target="tpu_custom_call" | custom-call | tf_op jit(solution)/shard_map/pallas_call | solution.py:700
  77.7 2.5 %copy.9 = bf16[4,16,64,128]{3,2,1,0:T(8,128)(2,1)} copy(bf16[4,16,64,128]{3,1,2,0:T(8,128)(2,1)} %bitcast.3) | data formatting | bytes 2097152 | tf_op jit(solution)/shard_map/transpose | solution.py:691

commit v6 on v4

--- a/solution.py
+++ b/solution.py
@@ -308,23 +308,25 @@
         def plain(piece):
             return isinstance(piece[2], int) and piece[2] < skip
 
-        def each(piece, down, down_split, up, up_split):
+        def each(piece, down, down_split, up, up_split, middle=True, others=True):
             if plain(piece):
                 pl.when(has_down)(down)
                 pl.when(has_up)(up)
                 return
-            pl.when(jnp.logical_and(has_down, lt != HALF - 1))(down)
-            pl.when(lt == HALF - 1)(down_split)
-            pl.when(jnp.logical_and(has_up, lt != HALF))(up)
-            pl.when(lt == HALF)(up_split)
-
-        def start(*piece):
+            if others:
+                pl.when(jnp.logical_and(has_down, lt != HALF - 1))(down)
+                pl.when(jnp.logical_and(has_up, lt != HALF))(up)
+            if middle:
+                pl.when(lt == HALF - 1)(down_split)
+                pl.when(lt == HALF)(up_split)
+
+        def start(*piece, **which):
             def split(way):
                 direct(way, 2, *piece).start()
                 lend(way, *piece).start()
 
             each(piece, lambda: direct(0, 3, *piece).start(), lambda: split(0),
-                 lambda: direct(1, 3, *piece).start(), lambda: split(1))
+                 lambda: direct(1, 3, *piece).start(), lambda: split(1), **which)
 
         def forward(*piece):
             @pl.when(lt == LAT_DEVICES - 1)
@@ -566,7 +568,7 @@
 
         if b == 0:
             h_start(*h_pieces[3])
-            h_start(*h_pieces[4])
+            h_start(*h_pieces[4], others=False)
             h_forward(*h_pieces[1])
         swap = pltpu.make_async_remote_copy(
             src_ref=PART.at[1 - core], dst_ref=DR.at[b],
@@ -645,6 +647,7 @@
         forward.start()
         if b == 0:
             g_start()
+            h_start(*h_pieces[4], middle=False)
         back = pltpu.make_async_remote_copy(
             src_ref=G.at[b, 1 - core], dst_ref=G.at[b, 1 - core],
             send_sem=fw_s.at[0], recv_sem=fw_r.at[b],

time: 80.4 us -> 80.4 us (level)
  no operation moved by 1% of the time
where the time goes in v6:
time: 80.4 us; the launch traced here: 80.2 us
  Pallas kernels  77.8 us (97%)
  local copies, waits for them, and re-layouts  2.47 us (3%)
    pallas_call x1, Pallas kernels, per_device(): pl.pallas_call(kernel, out_shape=jax.ShapeDtypeStruct((ROWS, TILES) + til...  77.8 us
    transpose x1, local copies, waits for them, and re-layouts, restore(): return jnp.transpose(strips, (0, 2, 1, 3)).reshape(ROWS, COLS, CH)  2.47 us

profile of v6, /device:TPU:25, one launch (start us, length us, event | category | flops | bytes accessed | tf_op | source)
XLA Modules:
  0.0 80.2 jit_solution(13930210006598517375)
XLA Ops:
  0.0 77.8 %shard_map.82 = bf16[4,64,16,128]{3,2,1,0:T(8,128)(2,1)} custom-call(bf16[4,1024,128]{2,1,0:T(8,128)(2,1)} %field.1, bf16[2,3,3,3,128,128]{5,4,3,2,1,0:T(8,128)(2,1)} %cw.1, f32[3,2,128]{2,1,0:T(2,128)} %bitcast.4, bf16[2,8,128,128]{3,2,1,0:T(8,128)(2,1)} %sr.1, bf16[2,8,128,128]{3,2,1,0:T(8,128)(2,1)} %si.1, bf16[512,1024]{1,0:T(8,128)(2,1)} %constant.6.clone.ft, ...), custom_call_target="tpu_custom_call" | custom-call | tf_op jit(solution)/shard_map/pallas_call | solution.py:701
  77.8 2.5 %copy.9 = bf16[4,16,64,128]{3,2,1,0:T(8,128)(2,1)} copy(bf16[4,16,64,128]{3,1,2,0:T(8,128)(2,1)} %bitcast.3) | data formatting | bytes 2097152 | tf_op jit(solution)/shard_map/transpose | solution.py:692

commit v7 on v5

--- a/solution.py
+++ b/solution.py
@@ -404,13 +404,13 @@
         return jnp.concatenate([hi, hi, lo], axis=0)
 
     def inverse(c, rhs):
-        table = iv_v[pl.ds(c * 512, 512), :]
+        table = iv_v[...]
         lhs = jnp.concatenate([table, table[:, 0:256]], axis=1)
         return jnp.dot(lhs, rhs, preferred_element_type=F32)
 
     def result(c, l):
         return pltpu.make_async_copy(
-            X.at[BLOCKS, 3 + l, pl.ds(3 + 32 * c, 32)], out.at[l, pl.ds(32 * c, 32)],
+            X.at[BLOCKS, 3 + l, pl.ds(3, 64)], out.at[l],
             in_sem.at[4 * c + l])
 
     x_pieces = ([(9, 11, 0)] + [(20 + 9 * k, 9, k + 1) for k in range(5)]
@@ -508,20 +508,20 @@
 
         def rows(c, _):
             spectral = inverse(c, rhs)
-            tiles = pl.ds(3 + 32 * c, 32)
+            tiles = pl.ds(3, 64)
             for side, present in ((0, has_up), (1, has_down)):
                 @pl.when(present)
                 def _():
                     for l in range(3):
-                        x = X[0, 7 * side + l, tiles].reshape(512, CH).astype(F32)
-                        h = HH[3 * side + l, tiles].reshape(512, CH).astype(F32)
+                        x = X[0, 7 * side + l, tiles].reshape(1024, CH).astype(F32)
+                        h = HH[3 * side + l, tiles].reshape(1024, CH).astype(F32)
                         lanes = slice((3 * side + l) * CH, (3 * side + l + 1) * CH)
                         value = jnp.tanh(x + h + spectral[:, lanes])
-                        X[1, 7 * side + l, tiles] = value.astype(BF16).reshape(32, STRIPS, CH)
+                        X[1, 7 * side + l, tiles] = value.astype(BF16).reshape(64, STRIPS, CH)
             return 0
 
         with scope("halorows"):
-            lax.fori_loop(0, 2, rows, 0)
+            rows(0, 0)
         top = lon_pair(1, 0, 3, 2)
         bottom = lon_pair(1, 7, 3, 3)
         for copy in top + bottom:
@@ -659,11 +659,11 @@
         def finish(c, _):
             spectral = inverse(c, rhs)
             for l in range(ROWS):
-                x = X[b, 3 + l, pl.ds(3 + 32 * c, 32)].reshape(512, CH).astype(F32)
-                h = H3[b, l, pl.ds(3 + 32 * c, 32)].reshape(512, CH).astype(F32)
+                x = X[b, 3 + l, pl.ds(3, 64)].reshape(1024, CH).astype(F32)
+                h = H3[b, l, pl.ds(3, 64)].reshape(1024, CH).astype(F32)
                 value = jnp.tanh(x + h + spectral[:, l * CH:(l + 1) * CH])
-                X[b + 1, 3 + l, pl.ds(3 + 32 * c, 32)] = value.astype(BF16).reshape(
-                    32, STRIPS, CH)
+                X[b + 1, 3 + l, pl.ds(3, 64)] = value.astype(BF16).reshape(
+                    64, STRIPS, CH)
                 if b == BLOCKS - 1:
                     result(c, l).start()
 
@@ -671,7 +671,7 @@
             return 0
 
         with scope("finish"):
-            lax.fori_loop(0, 2, finish, 0)
+            finish(0, 0)
 
         gathered.wait_send()
         forward.wait_send()
@@ -682,7 +682,7 @@
     spectral_part(1)
 
     with scope("store"):
-        for c in range(2):
+        for c in range(1):
             for l in range(ROWS):
                 result(c, l).wait()
 

time: 80.3 us -> 80.6 us (level)
  no operation moved by 1% of the time
where the time goes in v7:
time: 80.6 us; the launch traced here: 80.4 us
  Pallas kernels  78 us (97%)
  local copies, waits for them, and re-layouts  2.47 us (3%)
    pallas_call x1, Pallas kernels, per_device(): pl.pallas_call(kernel, out_shape=jax.ShapeDtypeStruct((ROWS, TILES) + til...  78 us
    transpose x1, local copies, waits for them, and re-layouts, restore(): return jnp.transpose(strips, (0, 2, 1, 3)).reshape(ROWS, COLS, CH)  2.47 us

profile of v7, /device:TPU:25, one launch (start us, length us, event | category | flops | bytes accessed | tf_op | source)
XLA Modules:
  0.0 80.4 jit_solution(2043628815753133233)
XLA Ops:
  0.0 78.0 %shard_map.82 = bf16[4,64,16,128]{3,2,1,0:T(8,128)(2,1)} custom-call(bf16[4,1024,128]{2,1,0:T(8,128)(2,1)} %field.1, bf16[2,3,3,3,128,128]{5,4,3,2,1,0:T(8,128)(2,1)} %cw.1, f32[3,2,128]{2,1,0:T(2,128)} %bitcast.4, bf16[2,8,128,128]{3,2,1,0:T(8,128)(2,1)} %sr.1, bf16[2,8,128,128]{3,2,1,0:T(8,128)(2,1)} %si.1, bf16[512,1024]{1,0:T(8,128)(2,1)} %constant.6.clone.ft, ...), custom_call_target="tpu_custom_call" | custom-call | tf_op jit(solution)/shard_map/pallas_call | solution.py:700
  78.0 2.5 %copy.9 = bf16[4,16,64,128]{3,2,1,0:T(8,128)(2,1)} copy(bf16[4,16,64,128]{3,1,2,0:T(8,128)(2,1)} %bitcast.3) | data formatting | bytes 2097152 | tf_op jit(solution)/shard_map/transpose | solution.py:691

commit v8 on v4

--- a/solution.py
+++ b/solution.py
@@ -642,9 +642,9 @@
             src_ref=G.at[b, core], dst_ref=G.at[b, core],
             send_sem=fw_s.at[0], recv_sem=fw_r.at[b],
             device_id={"lon": sibling}, device_id_type=MESH)
-        forward.start()
         if b == 0:
             g_start()
+        forward.start()
         back = pltpu.make_async_remote_copy(
             src_ref=G.at[b, 1 - core], dst_ref=G.at[b, 1 - core],
             send_sem=fw_s.at[0], recv_sem=fw_r.at[b],

time: 80.4 us -> 80.4 us (level)
  no operation moved by 1% of the time
where the time goes in v8:
time: 80.4 us; the launch traced here: 80.3 us
  Pallas kernels  77.8 us (97%)
  local copies, waits for them, and re-layouts  2.47 us (3%)
    pallas_call x1, Pallas kernels, per_device(): pl.pallas_call(kernel, out_shape=jax.ShapeDtypeStruct((ROWS, TILES) + til...  77.8 us
    transpose x1, local copies, waits for them, and re-layouts, restore(): return jnp.transpose(strips, (0, 2, 1, 3)).reshape(ROWS, COLS, CH)  2.47 us

profile of v8, /device:TPU:25, one launch (start us, length us, event | category | flops | bytes accessed | tf_op | source)
XLA Modules:
  0.0 80.3 jit_solution(5984876304139017776)
XLA Ops:
  0.0 77.8 %shard_map.82 = bf16[4,64,16,128]{3,2,1,0:T(8,128)(2,1)} custom-call(bf16[4,1024,128]{2,1,0:T(8,128)(2,1)} %field.1, bf16[2,3,3,3,128,128]{5,4,3,2,1,0:T(8,128)(2,1)} %cw.1, f32[3,2,128]{2,1,0:T(2,128)} %bitcast.4, bf16[2,8,128,128]{3,2,1,0:T(8,128)(2,1)} %sr.1, bf16[2,8,128,128]{3,2,1,0:T(8,128)(2,1)} %si.1, bf16[512,1024]{1,0:T(8,128)(2,1)} %constant.6.clone.ft, ...), custom_call_target="tpu_custom_call" | custom-call | tf_op jit(solution)/shard_map/pallas_call | solution.py:698
  77.8 2.5 %copy.9 = bf16[4,16,64,128]{3,2,1,0:T(8,128)(2,1)} copy(bf16[4,16,64,128]{3,1,2,0:T(8,128)(2,1)} %bitcast.3) | data formatting | bytes 2097152 | tf_op jit(solution)/shard_map/transpose | solution.py:689
